TPU v7x, 32 devices: a whole 2x2x4 slice. The times are simulated.
32 devices in a mesh: tm: 8 (over z, x), freq: 4 (over y, core).
Axes of the slice: x: 2, y: 2, z: 4, core: 2. Of those that a mesh axis runs over, the one named last changes fastest.
Arguments:
- waveform: float32 [1048576], P(('tm', 'freq')), may hold values from -24.5 to 24.5
- starts: int32 [4096], P(('tm', 'freq')), may hold values from 0 to 1048575, as said below
- templates: float32 [1024, 512], P('freq'), may hold values from 0.05 to 2
- activations: float32 [4096, 512], P('tm', 'freq'), may hold values from 0.05 to 2
Outputs:
- templates_out: float32 [1024, 512], P('freq')
- activations_out: float32 [4096, 512], P('tm', 'freq')
Inputs may be any that keep to these rules, and one draw needn't show every extreme that they name: Frame j starts within the stretch of 32768 samples numbered j // 128: (j // 128) * 32768 <= starts[j] < (j // 128 + 1) * 32768.
All inputs are finite; a program needn't handle non-finite values.
Results may differ from a plain program's by a relative error of at most 0.003.
The roundings to bfloat16 on the way count: a program that leaves them out, or rounds other values in their place, can miss the bound.
Values may be sent and summed in bfloat16 or wider, within the bound.
No kernel may reach another device: no remote copies, remote signals or barrier semaphores. Data moves between devices by JAX's collectives and lax.ppermute only.
A program may use at most 64 MiB of HBM per device.

v0:
```python
import functools
import math

import jax
import jax.numpy as jnp
import numpy as np
from jax import lax
from jax.experimental import pallas as pl
from jax.experimental.pallas import tpu as pltpu
from jax.sharding import PartitionSpec as P


ITERS = 2
TM, FREQ = "tm", "freq"
LANES = 128
AUX = 16
BF16 = jnp.bfloat16
F32 = jnp.float32
VMEM = pl.BlockSpec(memory_space=pltpu.VMEM)
SMEM = pl.BlockSpec(memory_space=pltpu.SMEM)
HBM = pl.BlockSpec(memory_space=pltpu.HBM)

NT = (((1,), (1,)), ((), ()))
NN = (((1,), (0,)), ((), ()))


def dot(a, b, dims=NN):
    return lax.dot_general(a, b, dims, preferred_element_type=F32)


def split_rows(total):
    high = total.astype(BF16)
    low = (total - high.astype(F32)).astype(BF16)
    row = lax.broadcasted_iota(jnp.int32, (AUX, total.shape[1]), 0)
    rows = jnp.where(row == 0, high.astype(F32), jnp.where(row == 1, low.astype(F32), 0.0))
    return rows.astype(BF16)


def join_rows(block):
    both = block.astype(F32)
    return both[0:1, :] + both[1:2, :]


def stack_lanes(row):
    return jnp.concatenate([row[:, at : at + LANES] for at in range(0, row.shape[1], LANES)], axis=0)


def split_stack(total):
    high = total.astype(BF16).astype(F32)
    rest = jnp.zeros((AUX - 2 * total.shape[0], LANES), F32)
    return jnp.concatenate([high, total - high, rest], axis=0).astype(BF16)


def join_stack(block, lanes):
    both = block.astype(F32)
    return both[0:lanes, :] + both[lanes : 2 * lanes, :]


def call(body, out_shape, *args, in_specs=None, scratch=(), flops=0, nbytes=1 << 20, limit=40 << 20):
    return pl.pallas_call(
        body,
        out_shape=out_shape,
        in_specs=in_specs if in_specs is not None else [VMEM] * len(args),
        out_specs=jax.tree.map(lambda _: VMEM, out_shape),
        scratch_shapes=list(scratch),
        cost_estimate=pl.CostEstimate(flops=flops, bytes_accessed=nbytes, transcendentals=0),
        compiler_params=pltpu.CompilerParams(vmem_limit_bytes=limit),
    )(*args)


def shape(rows, cols, dtype):
    return jax.ShapeDtypeStruct((rows, cols), dtype)


def angle_tables(length, bins, step):
    k = np.arange(bins)[None, :]

    def angles(n):
        return (n[:, None] * k % length) * (2.0 * math.pi / length)

    coarse = angles(np.arange(length // 2 // step) * step)
    fine = angles(np.arange(step))
    return np.concatenate([np.cos(coarse), np.sin(coarse), np.cos(fine), np.sin(fine)]).astype(np.float32)


def hann_rows(length):
    window = 0.5 - 0.5 * np.cos(np.arange(length) * (2.0 * math.pi / length))
    return window.astype(np.float32).reshape(length // LANES, LANES)


def prepare(w_hbm, a_hbm, base_hbm, wave_hbm, pack_ref, base_ref, head_ref, w_ref, a_ref, sems):
    bins, width = w_ref.shape
    part = a_ref.shape[0] // 4
    own = a_ref.shape[1]
    core = lax.axis_index(FREQ) & 1
    blocks = [(other, side) for other in range(2) for side in range(2)]
    acts = []
    for index, (other, side) in enumerate(blocks):
        at = pl.ds(pl.multiple_of((2 * side + (core ^ other)) * part, part), part)
        to = slice(index * part, (index + 1) * part)
        acts.append(pltpu.make_async_copy(a_hbm.at[at], a_ref.at[to], sems.at[3 + index]))
    copies = [
        pltpu.make_async_copy(wave_hbm.at[0 : head_ref.shape[0]], head_ref, sems.at[0]),
        pltpu.make_async_copy(w_hbm, w_ref, sems.at[1]),
        pltpu.make_async_copy(base_hbm, base_ref, sems.at[2]),
    ]
    for copy in acts + copies:
        copy.start()
    for index, (other, side) in enumerate(blocks):
        acts[index].wait()
        to = slice(index * part, (index + 1) * part)
        cols = slice(width + other * own, width + (other + 1) * own)
        pack_ref[side * part : (side + 1) * part, cols] = a_ref[to, :].astype(BF16)
    copies[1].wait()
    w = w_ref[...]
    pack_ref[0:bins, 0:width] = w.astype(BF16)
    pack_ref[bins : bins + AUX, 0:width] = split_rows(jnp.sum(w, axis=0, keepdims=True))
    pack_ref[bins : bins + AUX, width:] = jnp.zeros((AUX, 2 * own), BF16)
    copies[0].wait()
    copies[2].wait()


def take_heads(own_ref, side_ref, both_ref, first_ref):
    tiles = own_ref.shape[0]
    side = lax.shift_right_logical(lax.axis_index(FREQ), 1)
    own, other = own_ref[...], side_ref[0:tiles, :]
    both_ref[0:tiles, :] = own
    both_ref[tiles : 2 * tiles, :] = other
    first_ref[...] = jnp.where(side == 0, own, other)


def join_packs(own_ref, side_ref, out_ref):
    rows, packed = own_ref.shape
    quarter = packed - out_ref.shape[1]
    width = packed - 2 * quarter
    for index, pack in enumerate((own_ref, side_ref)):
        at = slice(index * rows, (index + 1) * rows)
        out_ref[at, 0:width] = pack[:, 0:width]
        out_ref[at, width:] = pack[:, width + quarter :]


def build_table(base_ref, out_ref, *, step, block):
    coarse = out_ref.shape[0] // step
    place = lax.axis_index(FREQ)
    for turn in range(4):
        for part in range(0, block, LANES):
            cols = pl.ds(pl.multiple_of((place ^ turn) * block + part, LANES), LANES)
            c2 = base_ref[2 * coarse : 2 * coarse + step, cols]
            s2 = base_ref[2 * coarse + step : 2 * coarse + 2 * step, cols]
            cos_at = slice(turn * 2 * block + part, turn * 2 * block + part + LANES)
            sin_at = slice(cos_at.start + block, cos_at.stop + block)
            for n in range(coarse):
                c1 = base_ref[n : n + 1, cols]
                s1 = base_ref[coarse + n : coarse + n + 1, cols]
                rows = slice(n * step, (n + 1) * step)
                out_ref[rows, cos_at] = (c1 * c2 - s1 * s2).astype(BF16)
                out_ref[rows, sin_at] = (-(s1 * c2 + c1 * s2)).astype(BF16)


def cut_frames(
    own_starts, side_starts, own_wave, side_wave, heads_ref, *rest, segment, last,
):
    next_ref = rest[0] if last else None
    window_ref, out_ref, ext_ref, raw_ref = rest[-4:]
    tiles = window_ref.shape[0]
    count = own_starts.shape[0]
    wave_rows = own_wave.shape[0]
    place = lax.axis_index(FREQ)
    core, side = place & 1, lax.shift_right_logical(place, 1)
    mine = side == last
    ext_ref[0:wave_rows, :] = jnp.where(mine, own_wave[...], side_wave[...])
    own_head, side_head = heads_ref[0:tiles, :], heads_ref[tiles : 2 * tiles, :]
    same = jnp.where(mine, own_head, side_head)
    after = next_ref[...] if last else jnp.where(mine, side_head, own_head)
    ext_ref[wave_rows : wave_rows + tiles, :] = jnp.where(core == 0, same, after)
    lane = lax.broadcasted_iota(jnp.int32, (tiles, LANES), 1)
    window = window_ref[...]

    def body(i, carry):
        start = jnp.where(mine, own_starts[i], side_starts[i])
        start = start & (segment - 1) if segment & (segment - 1) == 0 else lax.rem(start, segment)
        row = lax.shift_right_logical(start, 7)
        shift = start & (LANES - 1)
        back = (LANES - shift) & (LANES - 1)
        first = pltpu.roll(ext_ref[pl.ds(row, tiles), :], back, 1)
        second = pltpu.roll(ext_ref[pl.ds(row + 1, tiles), :], back, 1)
        raw_ref[pl.ds(i, tiles, stride=count), :] = jnp.where(lane < LANES - shift, first, second) * window
        return carry

    lax.fori_loop(0, count, body, 0, unroll=32)
    half = tiles // 2
    for j in range(tiles):
        rows = slice((j // half) * count, (j // half + 1) * count)
        cols = slice((j % half) * LANES, (j % half + 1) * LANES)
        out_ref[rows, cols] = raw_ref[j * count : (j + 1) * count, :].astype(BF16)


def transform(front_ref, back_ref, table_ref, energy_ref, *rest, first):
    turned_ref, frames_ref = rest if len(rest) == 2 else (None, rest[0])
    per = front_ref.shape[0] // 2
    count = 2 * per
    for part in range(2):
        rows = slice(part * per, (part + 1) * per)
        frames_ref[part * count : part * count + per, :] = front_ref[rows, :]
        frames_ref[part * count + per : (part + 1) * count, :] = back_ref[rows, :]
    block = energy_ref.shape[1] // 2
    parity = lax.broadcasted_iota(jnp.int32, (1, 2 * block), 1) & 1
    sign = 1.0 - 2.0 * parity.astype(F32)
    for index in range(2):
        at = (first + index) * 2 * block
        both = dot(frames_ref[...], table_ref[:, at : at + 2 * block])
        whole = both[:count] + sign * both[count:]
        energy = (whole[:, :block] ** 2 + whole[:, block:] ** 2) * 0.25
        energy_ref[:, index * block : (index + 1) * block] = energy
        if turned_ref is not None:
            turned_ref[index * block : (index + 1) * block, :] = energy.T


def numerators(half_acts, energy_ref, templates, numerator=None, block=0):
    block = block or energy_ref.shape[1] // 2
    for index in range(templates.shape[0] // block):
        at = slice(index * block, (index + 1) * block)
        w = templates[at, :]
        ratios = (energy_ref[:, at] / dot(half_acts, w, NT)).astype(BF16)
        term = dot(ratios, w)
        numerator = term if numerator is None else numerator + term
    return numerator


def template_share(half_acts, turned_ref, w):
    ratios = (turned_ref[...] / dot(w, half_acts, NT)).astype(BF16)
    return dot(ratios, half_acts)


def finish_acts(acts, numerator, mass, turned_ref, w, send_ref, acts_ref, total_ref):
    block = w.shape[0]
    acts = acts * numerator / mass
    acts_ref[...] = acts
    half_acts = acts.astype(BF16)
    total = jnp.sum(half_acts.astype(F32), axis=0, keepdims=True)
    total_ref[...] = jnp.broadcast_to(total, total_ref.shape)
    send_ref[block : block + AUX, :] = split_rows(total)
    send_ref[0:block, :] = template_share(half_acts, turned_ref.at[block:], w).astype(BF16)


def own_share(acts_ref, turned_ref, w_ref, own_ref):
    block = own_ref.shape[0]
    own_ref[...] = template_share(acts_ref[...].astype(BF16), turned_ref.at[0:block], w_ref[0:block, :])


def own_acts(acts_ref, keep_ref, give_ref):
    quarter = keep_ref.shape[1]
    place = lax.axis_index(FREQ)
    keep_ref[...] = acts_ref[:, pl.ds(pl.multiple_of(place * quarter, LANES), quarter)]
    give_ref[...] = acts_ref[:, pl.ds(pl.multiple_of((place ^ 1) * quarter, LANES), quarter)]


def first_update(
    energy_ref, later_ref, turned_ref, own_pack, side_pack, other_pack,
    send_ref, acts_ref, total_ref, own_w_ref, w_ref, a_ref,
):
    block = energy_ref.shape[1] // 2
    width = w_ref.shape[1]
    quarter = width // 4
    count = a_ref.shape[0]
    pitch = block + AUX
    place = lax.axis_index(FREQ)
    mass = None
    for turn, (pack, base) in enumerate(((own_pack, 0), (other_pack, 0), (side_pack, 0), (other_pack, pitch))):
        w_ref[turn * block : (turn + 1) * block, :] = pack[base : base + block, 0:width]
        part = join_rows(pack[base + block : base + pitch, 0:width])
        mass = part if mass is None else mass + part
        cols = pl.ds(pl.multiple_of((place ^ turn) * quarter, LANES), quarter)
        a_ref[:, cols] = pack[base : base + count, width : width + quarter].astype(F32)
    acts = a_ref[...]
    half_acts = acts.astype(BF16)
    numerator = numerators(half_acts, energy_ref, w_ref.at[0 : 2 * block])
    numerator = numerators(half_acts, later_ref, w_ref.at[2 * block :], numerator)
    own_w_ref[...] = w_ref[0:block, :]
    finish_acts(acts, numerator, mass, turned_ref, w_ref[block : 2 * block, :], send_ref, acts_ref, total_ref)


def tm_bit(bit):
    return lax.shift_right_logical(lax.axis_index(TM), bit) & 1


def group_rows(chain, mine, quarter):
    bit = tm_bit(chain)
    return pl.ds(pl.multiple_of(2 * chain * quarter + (bit if mine else 1 - bit) * quarter, AUX), quarter)


def unpack_templates(pieces, w_ref):
    block = 2 * w_ref.shape[0] // len(pieces)
    width = w_ref.shape[1]
    lanes = width // LANES
    rows = block // 4
    pitch = lanes * rows + AUX
    mass = None
    for index, piece in enumerate(pieces):
        turn, mine = index // 2, index % 2 == 0
        for chain in range(2):
            at = group_rows(chain, mine, rows)
            at = pl.ds(pl.multiple_of(turn * block + at.start, AUX), rows)
            base = chain * pitch
            for lane in range(lanes):
                value = piece[base + lane * rows : base + (lane + 1) * rows, :]
                w_ref[at, lane * LANES : (lane + 1) * LANES] = value
            part = join_stack(piece[base + lanes * rows : base + pitch, :], lanes)
            mass = part if mass is None else mass + part
    return jnp.concatenate([mass[lane : lane + 1, :] for lane in range(lanes)], axis=1)


def early_update(energy_ref, a_ref, mine_ref, others_ref, core_ref, w_ref, numerator_ref, mass_ref):
    size = mine_ref.shape[0]
    pieces = mine_ref, others_ref, core_ref.at[0:size], core_ref.at[size:]
    mass_ref[...] = jnp.broadcast_to(unpack_templates(pieces, w_ref), mass_ref.shape)
    numerator_ref[...] = numerators(a_ref[...].astype(BF16), energy_ref, w_ref)


def middle_update(energy_ref, a_ref, numerator_ref, mass_ref, mine_ref, others_ref, more_ref, more_mass, w_ref):
    more_mass[...] = mass_ref[...] + unpack_templates((mine_ref, others_ref), w_ref)
    more_ref[...] = numerators(a_ref[...].astype(BF16), energy_ref, w_ref, numerator_ref[...])


def later_update(
    energy_ref, turned_ref, a_ref, early_ref, numerator_ref, mass_ref, mine_ref, others_ref,
    send_ref, acts_ref, total_ref, w_ref,
):
    block = w_ref.shape[0]
    mass = mass_ref[0:1, :] + unpack_templates((mine_ref, others_ref), w_ref)
    acts = a_ref[...]
    numerator = numerators(acts.astype(BF16), energy_ref.at[:, block:], w_ref, numerator_ref[...], block)
    finish_acts(acts, numerator, mass, turned_ref, early_ref[block:, :], send_ref, acts_ref, total_ref)


def add_core(own_ref, total_ref, got_ref, keep_a, keep_b, send_a, send_b):
    block, width = own_ref.shape
    rows = block // 4
    lanes = width // LANES
    for chain, (keep, send) in enumerate(((keep_a, send_a), (keep_b, send_b))):
        for ref, mine in ((keep, True), (send, False)):
            at = group_rows(chain, mine, rows)
            for lane in range(lanes):
                cols = slice(lane * LANES, (lane + 1) * LANES)
                value = own_ref[at, cols] + got_ref[at, cols].astype(F32)
                ref[lane * rows : (lane + 1) * rows, :] = value.astype(ref.dtype)
    total = stack_lanes(total_ref[0:1, :] + join_rows(got_ref[block : block + AUX, :]))
    aux = split_stack(total)
    keep_a[lanes * rows :, :] = aux.astype(F32)
    send_a[lanes * rows :, :] = aux


def add_blocks(mine, got, lanes):
    size = mine.shape[0] - AUX if lanes else mine.shape[0]
    total = mine[0:size, :].astype(F32) + got[0:size, :].astype(F32)
    if not lanes:
        return total, None
    return total, join_stack(mine[size:, :], lanes) + join_stack(got[size:, :], lanes)


def add_pair(mine_ref, got_ref, out_ref, *, lanes):
    total, aux = add_blocks(mine_ref, got_ref, lanes)
    out_ref[0 : total.shape[0], :] = total.astype(BF16)
    if lanes:
        out_ref[total.shape[0] :, :] = split_stack(aux)


def add_chains(a_ref, got_a, b_ref, got_b, out_ref, *, lanes):
    a, aux = add_blocks(a_ref, got_a, lanes)
    b, _ = add_blocks(b_ref, got_b, 0)
    size = b.shape[0]
    out_ref[0:size, :] = a.astype(BF16)
    out_ref[size : 2 * size, :] = b.astype(BF16)
    out_ref[2 * size :, :] = split_stack(aux)


def first_templates(w_ref, mine_ref, got_ref, new_a, new_b, send_a, send_b, both_ref):
    block, width = w_ref.shape
    rows = block // 4
    lanes = width // LANES
    size = lanes * rows
    numerator, total = add_blocks(mine_ref, got_ref, lanes)
    for chain, (new, send) in enumerate(((new_a, send_a), (new_b, send_b))):
        sums = []
        for lane in range(lanes):
            old = w_ref[group_rows(chain, True, rows), lane * LANES : (lane + 1) * LANES]
            at = slice(lane * rows, (lane + 1) * rows)
            value = old * numerator[chain * size + at.start : chain * size + at.stop] / total[lane : lane + 1, :]
            new[at, :] = value
            send[at, :] = value.astype(BF16)
            sums.append(jnp.sum(value, axis=0, keepdims=True))
        send[size:, :] = split_stack(jnp.concatenate(sums, axis=0))
        both_ref[chain * (size + AUX) : (chain + 1) * (size + AUX), :] = send[...]


def last_templates(old_a, old_b, mine_ref, got_ref, new_a, new_b, *, lanes):
    numerator, total = add_blocks(mine_ref, got_ref, lanes)
    size = old_a.shape[0]
    rows = size // lanes
    for chain, (old, new) in enumerate(((old_a, new_a), (old_b, new_b))):
        for lane in range(lanes):
            at = slice(lane * rows, (lane + 1) * rows)
            value = numerator[chain * size + at.start : chain * size + at.stop]
            new[at, :] = old[at, :] * value / total[lane : lane + 1, :]


def join_groups(mine_ref, a_ref, b_ref, others_ref, all_ref):
    size = a_ref.shape[0]
    for index, ref in enumerate((a_ref, b_ref)):
        others_ref[index * size : (index + 1) * size, :] = ref[...]
        all_ref[(2 + index) * size : (3 + index) * size, :] = ref[...]
    all_ref[0 : 2 * size, :] = mine_ref[...]


def place_acts(keep_ref, given_ref, first_ref, a_out):
    part = keep_ref.shape[0] // 2
    core = lax.axis_index(FREQ) & 1
    for side in range(2):
        rows = slice(side * part, (side + 1) * part)
        for value, which in ((keep_ref, core), (given_ref, 1 - core)):
            at = pl.ds(pl.multiple_of((2 * side + which) * part, part), part)
            first = first_ref[at, :]
            a_out[at, :] = value[rows, :] * (first / first.astype(BF16).astype(F32))


def place_templates(mine_a, mine_b, got_a, got_b, w_out):
    rows = w_out.shape[0] // 4
    for chain, (mine, got) in enumerate(((mine_a, got_a), (mine_b, got_b))):
        for ref, own in ((mine, True), (got, False)):
            for lane in range(w_out.shape[1] // LANES):
                cols = slice(lane * LANES, (lane + 1) * LANES)
                w_out[group_rows(chain, own, rows), cols] = ref[lane * rows : (lane + 1) * rows, :]


def swap(block, axis, bit):
    return lax.ppermute(block, axis, [(i, i ^ bit) for i in range(lax.axis_size(axis))])


def shards(waveform, starts, templates, activations):
    tm, freq = lax.axis_size(TM), lax.axis_size(FREQ)
    block, width = templates.shape
    count = activations.shape[0] // 2
    bins = block * freq
    segment = waveform.shape[0]
    per = starts.shape[0]
    quarter = activations.shape[1]
    length = 2048
    tiles = length // LANES
    step = 32
    assert freq == 4 and tm >= 8 and tm & (tm - 1) == 0

    wave = waveform.reshape(segment // LANES, LANES)
    side_wave = swap(wave, FREQ, 2)
    side_starts = swap(starts, FREQ, 2)

    base = jnp.asarray(angle_tables(length, bins, step))
    pitch = block + AUX
    pack, base, head = call(
        prepare,
        (shape(pitch, width + 2 * quarter, BF16), shape(*base.shape, F32), shape(tiles, LANES, F32)),
        *(pltpu.with_memory_space_constraint(x, pltpu.HBM) for x in (templates, activations, base, wave)),
        in_specs=[HBM] * 4,
        scratch=[pltpu.VMEM(templates.shape, F32), pltpu.VMEM(activations.shape, F32), pltpu.SemaphoreType.DMA((7,))],
    )
    pack_y = swap(pack, FREQ, 2)
    table = call(
        functools.partial(build_table, step=step, block=block),
        shape(length // 2, 2 * bins, BF16), base, flops=4 << 20, nbytes=8 << 20,
    )
    heads, first = call(
        take_heads, (shape(2 * tiles, LANES, F32), shape(tiles, LANES, F32)), head, side_wave,
    )
    heads = swap(heads, FREQ, 1)
    route = [((t + 1) * freq + f, t * freq + f + 1) for t in range(tm - 1) for f in range(0, freq, 2)]
    following = lax.ppermute(first, (TM, FREQ), route)
    joined = call(join_packs, shape(2 * pitch, width + quarter, BF16), pack, pack_y)
    joined = swap(joined, FREQ, 1)

    window = jnp.asarray(hann_rows(length))
    frames = []
    for last in range(2):
        follow = (following,) if last else ()
        frames.append(
            call(
                functools.partial(cut_frames, segment=segment, last=last), shape(2 * per, length // 2, BF16),
                starts, side_starts, wave, side_wave, heads, *follow, window,
                in_specs=[SMEM] * 2 + [VMEM] * (4 + last),
                scratch=[
                    pltpu.VMEM((segment // LANES + tiles, LANES), F32), pltpu.VMEM((tiles * per, LANES), F32),
                ],
                nbytes=4 << 20,
            )
        )
    energies = []
    for index in range(2):
        more = (shape(2 * block, count, F32),) if index == 0 else ()
        energies += call(
            functools.partial(transform, first=2 * index), (shape(count, 2 * block, F32),) + more,
            *frames, table, scratch=[pltpu.VMEM((2 * count, length // 2), BF16)],
            flops=2 * count * length * bins, nbytes=8 << 20,
        )
    energy, turned, later_energy = energies

    outs = (shape(block + AUX, width, BF16), shape(count, width, F32), shape(8, width, F32))
    work = 3 * 2 * count * bins * width
    acts = pieces = None
    lanes = width // LANES
    size = lanes * block // 4
    for iteration in range(ITERS):
        if iteration == 0:
            send, acts, total, weights = call(
                first_update, outs + (shape(block, width, BF16),), energy, later_energy, turned, pack, pack_y, joined,
                scratch=[pltpu.VMEM((bins, width), BF16), pltpu.VMEM((count, width), F32)], flops=work,
                nbytes=4 << 20,
            )
        else:
            sums = shape(count, width, F32), shape(8, width, F32)
            weights, numerator, mass = call(
                early_update, (shape(2 * block, width, BF16),) + sums, energy, acts, *pieces[:3],
                flops=work // 3,
            )
            numerator, mass = call(
                middle_update, sums, later_energy, acts, numerator, mass, *pieces[3:5],
                scratch=[pltpu.VMEM((block, width), BF16)], flops=work // 6,
            )
            send, acts, total = call(
                later_update, outs, later_energy, turned, acts, weights, numerator, mass, *pieces[5:],
                scratch=[pltpu.VMEM((block, width), BF16)], flops=work // 2, nbytes=4 << 20,
            )
        got = swap(send, FREQ, 1)
        own = call(own_share, shape(block, width, F32), acts, turned, weights, flops=work // 6)
        if iteration == ITERS - 1:
            keep_acts, give_acts = call(own_acts, (shape(count, quarter, F32),) * 2, acts)
            given = swap(give_acts, FREQ, 1)
        sent = shape(size + AUX, LANES, BF16), shape(size, LANES, BF16)
        keep_a, keep_b, send_a, send_b = call(
            add_core, (shape(size + AUX, LANES, F32), shape(size, LANES, F32)) + sent, own, total, got,
        )
        got_a, got_b = swap(send_a, TM, 1), swap(send_b, TM, 2)
        send_a = call(functools.partial(add_pair, lanes=lanes), sent[0], keep_a, got_a)
        send_b = call(functools.partial(add_pair, lanes=0), sent[1], keep_b, got_b)
        got_a, got_b = swap(send_a, TM, 2), swap(send_b, TM, 1)
        both = shape(2 * size + AUX, LANES, BF16)
        mine = call(functools.partial(add_chains, lanes=lanes), both, send_a, got_a, send_b, got_b)
        bit = 4
        while bit < tm:
            if bit > 4:
                mine = call(functools.partial(add_pair, lanes=lanes), both, mine, got)
            got = swap(mine, TM, bit)
            bit *= 2
        part = shape(size, LANES, F32)
        if iteration < ITERS - 1:
            kept_a, kept_b, send_a, send_b, pieces = call(
                first_templates,
                (part, part, sent[0], sent[0], shape(2 * (size + AUX), LANES, BF16)), templates, mine, got,
            )
            other_a, other_b = swap(send_a, TM, 1), swap(send_b, TM, 2)
            pair = shape(2 * (size + AUX), LANES, BF16), shape(4 * (size + AUX), LANES, BF16)
            others, both_groups = call(join_groups, pair, pieces, other_a, other_b)
            in_y = [swap(pieces, FREQ, 2)]
            in_y.append(swap(others, FREQ, 2))
            in_core = swap(both_groups, FREQ, 1)
            pieces = [pieces, others, in_core] + in_y
            pieces.append(swap(in_y[0], FREQ, 1))
            pieces.append(swap(in_y[1], FREQ, 1))
        else:
            new_a, new_b = call(
                functools.partial(last_templates, lanes=lanes), (part, part), kept_a, kept_b, mine, got,
            )
            other_a = swap(new_a, TM, 1)
            other_b = swap(new_b, TM, 2)
            acts = call(
                place_acts, shape(2 * count, quarter, F32), keep_acts, given, activations,
            )
            weights = call(
                place_templates, shape(block, width, F32), new_a, new_b, other_a, other_b,
            )
            return weights, acts


def solution(mesh):
    in_specs = (P((TM, FREQ)), P((TM, FREQ)), P(FREQ, None), P(TM, FREQ))
    out_specs = (P(FREQ, None), P(TM, FREQ))
    return jax.shard_map(shards, mesh=mesh, in_specs=in_specs, out_specs=out_specs, check_vma=False)
```

profile of v0, /device:TPU:0, one launch (start us, length us, event | category | flops | bytes accessed | tf_op | source)
XLA Modules:
  0.0 98.8 jit_solution(776770275549311013)
XLA Ops:
  0.6 0.0 copy-start.3
  0.7 0.0 copy-start.4
  0.7 1.5 %shard_map.77 = (bf16[272,768]{1,0:T(8,128)(2,1)S(1)}, f32[128,1024]{1,0:T(8,128)S(1)}, f32[16,128]{1,0:T(8,128)S(1)}) custom-call(f32[256,512]{1,0:T(8,128)} %w_ref.1, f32[512,128]{1,0:T(8,128)} %first_ref.1, f32[128,1024]{1,0:T(8,128)} %constant.4.clone.base_hbm, f32[256,128]{1,0:T(8,128)} %bitcast.1), custom_call_target="tpu_custom_call" | custom-call | bytes 1048576 | tf_op jit(solution)/shard_map/pallas_call | solution.py:60
  2.1 3.1 %collective-permute-start.4 = (bf16[272,768]{1,0:T(8,128)(2,1)S(1)}, bf16[272,768]{1,0:T(8,128)(2,1)S(1)}, u32[]{:S(2)}, u32[]{:S(2)}) collective-permute-start(bf16[272,768]{1,0:T(8,128)(2,1)S(1)} %get-tuple-element.46.own_ref.own_pack), channel_id=1, source_target_pairs={{0,2},{1,3},{2,0},{3,1},{4,6},{5,7},{6,4},{7,5},{8,10},{9,11},{10,... | collective-permute-start | bytes 1253384 | tf_op jit(solution)/shard_map/ppermute | solution.py:436
  5.2 9.6 %collective-permute-done.4.side_ref.side_pack = bf16[272,768]{1,0:T(8,128)(2,1)S(1)} collective-permute-done((bf16[272,768]{1,0:T(8,128)(2,1)S(1)}, bf16[272,768]{1,0:T(8,128)(2,1)S(1)}, u32[]{:S(2)}, u32[]{:S(2)}) %collective-permute-start.4) | collective-permute-done | bytes 417824 | tf_op jit(solution)/shard_map/ppermute | solution.py:436
  14.8 0.1 shard_map.84
  14.9 0.1 collective-permute-start.5
  15.0 1.8 %collective-permute-start.1 = (f32[256,128]{1,0:T(8,128)}, f32[256,128]{1,0:T(8,128)S(1)}, u32[]{:S(2)}, u32[]{:S(2)}) collective-permute-start(f32[256,128]{1,0:T(8,128)} %bitcast.2), channel_id=1, source_target_pairs={{0,2},{1,3},{2,0},{3,1},{4,6},{5,7},{6,4},{7,5},{8,10},{9,11},{10,... | collective-permute-start | bytes 393224 | tf_op jit(solution)/shard_map/ppermute | solution.py:436
  16.8 4.3 %collective-permute-done.1.side_ref.side_wave = f32[256,128]{1,0:T(8,128)S(1)} collective-permute-done((f32[256,128]{1,0:T(8,128)}, f32[256,128]{1,0:T(8,128)S(1)}, u32[]{:S(2)}, u32[]{:S(2)}) %collective-permute-start.1) | collective-permute-done | bytes 131104 | tf_op jit(solution)/shard_map/ppermute | solution.py:436
  21.1 0.7 collective-permute-start.3
  21.8 1.8 %collective-permute-start = (s32[128]{0:T(128)}, s32[128]{0:T(128)S(1)}, u32[]{:S(2)}, u32[]{:S(2)}) collective-permute-start(s32[128]{0:T(128)} %own_starts.3), channel_id=1, source_target_pairs={{0,2},{1,3},{2,0},{3,1},{4,6},{5,7},{6,4},{7,5},{8,10},{9,11},{10,... | collective-permute-start | bytes 1544 | tf_op jit(solution)/shard_map/ppermute | solution.py:436
  23.6 1.3 %shard_map.81.table_ref = bf16[1024,2048]{1,0:T(8,128)(2,1)S(1)} custom-call(f32[128,1024]{1,0:T(8,128)S(1)} %get-tuple-element.43.base_ref), custom_call_target="tpu_custom_call" | custom-call | flops 4194304 | bytes 8388608 | tf_op jit(solution)/shard_map/pallas_call | solution.py:60
  24.9 0.7 collective-permute-done.side_starts
  25.6 1.9 %shard_map.79.front_ref = bf16[256,1024]{1,0:T(8,128)(2,1)S(1)} custom-call(s32[128]{0:T(128)S(1)} %copy-done.4, s32[128]{0:T(128)S(1)} %collective-permute-done.side_starts, f32[256,128]{1,0:T(8,128)S(1)} %bitcast.3, f32[256,128]{1,0:T(8,128)S(1)} %collective-permute-done.1.side_ref.side_wave, f32[32,128]{1,0:T(8,128)S(1)} %collective-permute-done.2.heads_ref, ...), custom_call_target="tpu_custom_call" | custom-call | bytes 4194304 | tf_op jit(solution)/shard_map/pallas_call | solution.py:60
  27.4 1.9 %shard_map.80.back_ref = bf16[256,1024]{1,0:T(8,128)(2,1)S(1)} custom-call(s32[128]{0:T(128)S(1)} %copy-done.4, s32[128]{0:T(128)S(1)} %collective-permute-done.side_starts, f32[256,128]{1,0:T(8,128)S(1)} %bitcast.4, f32[256,128]{1,0:T(8,128)S(1)} %collective-permute-done.1.side_ref.side_wave, f32[32,128]{1,0:T(8,128)S(1)} %collective-permute-done.2.heads_ref, ...), custom_call_target="tpu_custom_call" | custom-call | bytes 4194304 | tf_op jit(solution)/shard_map/pallas_call | solution.py:60
  29.3 1.3 %shard_map.82 = (f32[256,512]{1,0:T(8,128)S(1)}, f32[512,256]{1,0:T(8,128)S(1)}) custom-call(bf16[256,1024]{1,0:T(8,128)(2,1)S(1)} %shard_map.79.front_ref, bf16[256,1024]{1,0:T(8,128)(2,1)S(1)} %shard_map.80.back_ref, bf16[1024,2048]{1,0:T(8,128)(2,1)S(1)} %shard_map.81.table_ref), custom_call_target="tpu_custom_call" | custom-call | flops 1073741824 | bytes 8388608 | tf_op jit(solution)/shard_map/pallas_call | solution.py:60
  30.6 1.3 %shard_map.83.later_ref.energy_ref = f32[256,512]{1,0:T(8,128)S(1)} custom-call(bf16[256,1024]{1,0:T(8,128)(2,1)S(1)} %shard_map.79.front_ref, bf16[256,1024]{1,0:T(8,128)(2,1)S(1)} %shard_map.80.back_ref, bf16[1024,2048]{1,0:T(8,128)(2,1)S(1)} %shard_map.81.table_ref), custom_call_target="tpu_custom_call" | custom-call | flops 1073741824 | bytes 8388608 | tf_op jit(solution)/shard_map/pallas_call | solution.py:60
  31.9 1.6 %shard_map.85 = (bf16[272,512]{1,0:T(8,128)(2,1)S(1)}, f32[256,512]{1,0:T(8,128)S(1)}, f32[8,512]{1,0:T(8,128)S(1)}, bf16[256,512]{1,0:T(8,128)(2,1)S(1)}) custom-call(f32[256,512]{1,0:T(8,128)S(1)} %get-tuple-element.44.energy_ref, f32[256,512]{1,0:T(8,128)S(1)} %shard_map.83.later_ref.energy_ref, f32[512,256]{1,0:T(8,128)S(1)} %get-tuple-element.45.turned_ref, ...), custom_call_target="tpu_custom_call" | custom-call | flops 805306368 | bytes 4194304 | tf_op jit(solution)/shard_map/pallas_call | solution.py:60
  33.6 0.3 collective-permute-start.6
  33.8 0.5 shard_map.86.own_ref
  34.3 0.9 collective-permute-done.6.got_ref
  35.2 0.1 shard_map.87
  35.3 3.4 %collective-permute-start.7 = (bf16[272,128]{1,0:T(8,128)(2,1)S(1)}, bf16[272,128]{1,0:T(8,128)(2,1)S(1)}, u32[]{:S(2)}, u32[]{:S(2)}) collective-permute-start(bf16[272,128]{1,0:T(8,128)(2,1)S(1)} %get-tuple-element.52), channel_id=1, source_target_pairs={{0,4},{4,0},{8,12},{12,8},{16,20},{20,16},{24,28},{28,24},{1,5},{5... | collective-permute-start | bytes 208904 | tf_op jit(solution)/shard_map/ppermute | solution.py:436
  38.7 1.8 %collective-permute-start.9 = (bf16[256,128]{1,0:T(8,128)(2,1)S(1)}, bf16[256,128]{1,0:T(8,128)(2,1)S(1)}, u32[]{:S(2)}, u32[]{:S(2)}) collective-permute-start(bf16[256,128]{1,0:T(8,128)(2,1)S(1)} %get-tuple-element.54), channel_id=1, source_target_pairs={{0,8},{4,12},{8,0},{12,4},{16,24},{20,28},{24,16},{28,20},{1,9},{5... | collective-permute-start | bytes 196616 | tf_op jit(solution)/shard_map/ppermute | solution.py:436
  40.5 0.7 collective-permute-done.7.got_ref
  41.2 3.0 %collective-permute-start.8 = (bf16[272,128]{1,0:T(8,128)(2,1)S(1)}, bf16[272,128]{1,0:T(8,128)(2,1)S(1)}, u32[]{:S(2)}, u32[]{:S(2)}) collective-permute-start(bf16[272,128]{1,0:T(8,128)(2,1)S(1)} %shard_map.88.a_ref), channel_id=1, source_target_pairs={{0,8},{4,12},{8,0},{12,4},{16,24},{20,28},{24,16},{28,20},{1,9},{5... | collective-permute-start | bytes 208904 | tf_op jit(solution)/shard_map/ppermute | solution.py:436
  44.3 0.7 collective-permute-start.10
  45.0 3.6 %collective-permute-done.10.got_b = bf16[256,128]{1,0:T(8,128)(2,1)S(1)} collective-permute-done((bf16[256,128]{1,0:T(8,128)(2,1)S(1)}, bf16[256,128]{1,0:T(8,128)(2,1)S(1)}, u32[]{:S(2)}, u32[]{:S(2)}) %collective-permute-start.10) | collective-permute-done | bytes 65568 | tf_op jit(solution)/shard_map/ppermute | solution.py:436
  48.6 2.7 %collective-permute-start.11 = (bf16[528,128]{1,0:T(8,128)(2,1)S(1)}, bf16[528,128]{1,0:T(8,128)(2,1)S(1)}, u32[]{:S(2)}, u32[]{:S(2)}) collective-permute-start(bf16[528,128]{1,0:T(8,128)(2,1)S(1)} %shard_map.90.mine_ref), channel_id=1, source_target_pairs={{0,16},{4,20},{8,24},{12,28},{16,0},{20,4},{24,8},{28,12},{1,17},{... | collective-permute-start | bytes 405512 | tf_op jit(solution)/shard_map/ppermute | solution.py:436
  51.3 4.7 %collective-permute-done.11.got_ref = bf16[528,128]{1,0:T(8,128)(2,1)S(1)} collective-permute-done((bf16[528,128]{1,0:T(8,128)(2,1)S(1)}, bf16[528,128]{1,0:T(8,128)(2,1)S(1)}, u32[]{:S(2)}, u32[]{:S(2)}) %collective-permute-start.11) | collective-permute-done | bytes 135200 | tf_op jit(solution)/shard_map/ppermute | solution.py:436
  56.0 0.1 shard_map.91
  56.2 0.8 collective-permute-start.12
  56.9 0.5 collective-permute-start.13
  57.4 3.2 %collective-permute-done.12.a_ref = bf16[272,128]{1,0:T(8,128)(2,1)S(1)} collective-permute-done((bf16[272,128]{1,0:T(8,128)(2,1)S(1)}, bf16[272,128]{1,0:T(8,128)(2,1)S(1)}, u32[]{:S(2)}, u32[]{:S(2)}) %collective-permute-start.12) | collective-permute-done | bytes 69664 | tf_op jit(solution)/shard_map/ppermute | solution.py:436
  60.5 0.7 collective-permute-done.13.b_ref
  61.3 0.1 collective-permute-start.14
  61.3 1.6 %collective-permute-start.15 = (bf16[544,128]{1,0:T(8,128)(2,1)S(1)}, bf16[544,128]{1,0:T(8,128)(2,1)S(1)}, u32[]{:S(2)}, u32[]{:S(2)}) collective-permute-start(bf16[544,128]{1,0:T(8,128)(2,1)S(1)} %get-tuple-element.57.mine_ref), channel_id=1, source_target_pairs={{0,2},{1,3},{2,0},{3,1},{4,6},{5,7},{6,4},{7,5},{8,10},{9,11},{10,... | collective-permute-start | bytes 417800 | tf_op jit(solution)/shard_map/ppermute | solution.py:436
  62.9 0.5 collective-permute-start.16
  63.4 4.5 %collective-permute-done.15.mine_ref = bf16[544,128]{1,0:T(8,128)(2,1)S(1)} collective-permute-done((bf16[544,128]{1,0:T(8,128)(2,1)S(1)}, bf16[544,128]{1,0:T(8,128)(2,1)S(1)}, u32[]{:S(2)}, u32[]{:S(2)}) %collective-permute-start.15) | collective-permute-done | bytes 139296 | tf_op jit(solution)/shard_map/ppermute | solution.py:436
  68.0 2.4 %collective-permute-done.16.others_ref = bf16[544,128]{1,0:T(8,128)(2,1)S(1)} collective-permute-done((bf16[544,128]{1,0:T(8,128)(2,1)S(1)}, bf16[544,128]{1,0:T(8,128)(2,1)S(1)}, u32[]{:S(2)}, u32[]{:S(2)}) %collective-permute-start.16) | collective-permute-done | bytes 139296 | tf_op jit(solution)/shard_map/ppermute | solution.py:436
  70.4 0.7 shard_map.93
  71.1 0.5 shard_map.94
  71.6 0.1 collective-permute-done.18.others_ref
  71.8 0.9 shard_map.95
  72.7 0.5 collective-permute-start.19
  73.2 0.5 shard_map.96.own_ref
  73.7 0.7 collective-permute-done.19.got_ref
  74.3 0.1 shard_map.97
  74.4 1.4 %collective-permute-start.20 = (bf16[272,128]{1,0:T(8,128)(2,1)S(1)}, bf16[272,128]{1,0:T(8,128)(2,1)S(1)}, u32[]{:S(2)}, u32[]{:S(2)}) collective-permute-start(bf16[272,128]{1,0:T(8,128)(2,1)S(1)} %get-tuple-element.71), channel_id=1, source_target_pairs={{0,4},{4,0},{8,12},{12,8},{16,20},{20,16},{24,28},{28,24},{1,5},{5... | collective-permute-start | bytes 208904 | tf_op jit(solution)/shard_map/ppermute | solution.py:436
  75.8 3.1 %collective-permute-done.20.got_ref = bf16[272,128]{1,0:T(8,128)(2,1)S(1)} collective-permute-done((bf16[272,128]{1,0:T(8,128)(2,1)S(1)}, bf16[272,128]{1,0:T(8,128)(2,1)S(1)}, u32[]{:S(2)}, u32[]{:S(2)}) %collective-permute-start.20) | collective-permute-done | bytes 69664 | tf_op jit(solution)/shard_map/ppermute | solution.py:436
  78.9 0.5 collective-permute-start.21
  79.5 0.6 collective-permute-done.22.got_ref
  80.1 0.8 collective-permute-start.23
  80.8 3.6 %collective-permute-done.23.got_b = bf16[256,128]{1,0:T(8,128)(2,1)S(1)} collective-permute-done((bf16[256,128]{1,0:T(8,128)(2,1)S(1)}, bf16[256,128]{1,0:T(8,128)(2,1)S(1)}, u32[]{:S(2)}, u32[]{:S(2)}) %collective-permute-start.23) | collective-permute-done | bytes 65568 | tf_op jit(solution)/shard_map/ppermute | solution.py:436
  84.5 2.9 %collective-permute-start.24 = (bf16[528,128]{1,0:T(8,128)(2,1)S(1)}, bf16[528,128]{1,0:T(8,128)(2,1)S(1)}, u32[]{:S(2)}, u32[]{:S(2)}) collective-permute-start(bf16[528,128]{1,0:T(8,128)(2,1)S(1)} %shard_map.100.mine_ref), channel_id=1, source_target_pairs={{0,16},{4,20},{8,24},{12,28},{16,0},{20,4},{24,8},{28,12},{1,17},{... | collective-permute-start | bytes 405512 | tf_op jit(solution)/shard_map/ppermute | solution.py:436
  87.4 0.1 collective-permute-start.27
  87.4 4.6 %collective-permute-done.24.got_ref = bf16[528,128]{1,0:T(8,128)(2,1)S(1)} collective-permute-done((bf16[528,128]{1,0:T(8,128)(2,1)S(1)}, bf16[528,128]{1,0:T(8,128)(2,1)S(1)}, u32[]{:S(2)}, u32[]{:S(2)}) %collective-permute-start.24) | collective-permute-done | bytes 135200 | tf_op jit(solution)/shard_map/ppermute | solution.py:436
  92.1 0.1 shard_map.101
  92.1 0.8 collective-permute-start.25
  92.9 0.2 collective-permute-start.26
  93.2 0.8 shard_map.104
  93.9 3.2 %collective-permute-done.25.got_a = f32[256,128]{1,0:T(8,128)S(1)} collective-permute-done((f32[256,128]{1,0:T(8,128)S(1)}, f32[256,128]{1,0:T(8,128)S(1)}, u32[]{:S(2)}, u32[]{:S(2)}) %collective-permute-start.25) | collective-permute-done | bytes 131104 | tf_op jit(solution)/shard_map/ppermute | solution.py:436
  97.2 0.8 collective-permute-done.26.got_b
  97.9 0.8 shard_map.102
  (30 shorter events, 0.3 us)
Async XLA Ops:
  0.6 24.9 %copy-start.3 = (f32[16,128]{1,0:T(8,128)S(1)}, f32[16,128]{1,0:T(8,128)}, u32[]{:S(2)}) copy-start(f32[16,128]{1,0:T(8,128)} %constant.5.clone.rest_0_.rest_1_) | copy-start | bytes 24580
  0.6 24.9 %copy-start.1 = (f32[32768]{0:T(1024)S(1)}, f32[32768]{0:T(1024)}, u32[]{:S(2)}) copy-start(f32[32768]{0:T(1024)} %param.6) | copy-start | bytes 393220
  0.7 24.9 %copy-start.4 = (s32[128]{0:T(128)S(1)}, s32[128]{0:T(128)}, u32[]{:S(2)}) copy-start(s32[128]{0:T(128)} %own_starts.3) | copy-start | bytes 1540
  2.1 12.7 %collective-permute-start.4 = (bf16[272,768]{1,0:T(8,128)(2,1)S(1)}, bf16[272,768]{1,0:T(8,128)(2,1)S(1)}, u32[]{:S(2)}, u32[]{:S(2)}) collective-permute-start(bf16[272,768]{1,0:T(8,128)(2,1)S(1)} %get-tuple-element.46.own_ref.own_pack), channel_id=1, source_target_pairs={{0,2},{1,3},{2,0},{3,1},{4,6},{5,7},{6,4},{7,5},{8,10},{9,11},{10,... | collective-permute-start | bytes 1253384 | tf_op jit(solution)/shard_map/ppermute | solution.py:436
  14.9 17.0 %collective-permute-start.5 = (bf16[544,640]{1,0:T(8,128)(2,1)S(1)}, bf16[544,640]{1,0:T(8,128)(2,1)S(1)}, u32[]{:S(2)}, u32[]{:S(2)}) collective-permute-start(bf16[544,640]{1,0:T(8,128)(2,1)S(1)} %shard_map.84), channel_id=1, source_target_pairs={{0,1},{1,0},{2,3},{3,2},{4,5},{5,4},{6,7},{7,6},{8,9},{9,8},{10,11... | collective-permute-start | bytes 2088968 | tf_op jit(solution)/shard_map/ppermute | solution.py:436
  15.0 6.1 %collective-permute-start.1 = (f32[256,128]{1,0:T(8,128)}, f32[256,128]{1,0:T(8,128)S(1)}, u32[]{:S(2)}, u32[]{:S(2)}) collective-permute-start(f32[256,128]{1,0:T(8,128)} %bitcast.2), channel_id=1, source_target_pairs={{0,2},{1,3},{2,0},{3,1},{4,6},{5,7},{6,4},{7,5},{8,10},{9,11},{10,... | collective-permute-start | bytes 393224 | tf_op jit(solution)/shard_map/ppermute | solution.py:436
  21.1 4.4 %collective-permute-start.2 = (f32[32,128]{1,0:T(8,128)S(1)}, f32[32,128]{1,0:T(8,128)S(1)}, u32[]{:S(2)}, u32[]{:S(2)}) collective-permute-start(f32[32,128]{1,0:T(8,128)S(1)} %get-tuple-element.41), channel_id=1, source_target_pairs={{0,1},{1,0},{2,3},{3,2},{4,5},{5,4},{6,7},{7,6},{8,9},{9,8},{10,11... | collective-permute-start | bytes 49160 | tf_op jit(solution)/shard_map/ppermute | solution.py:436
  21.1 6.3 %collective-permute-start.3 = (f32[16,128]{1,0:T(8,128)S(1)}, f32[16,128]{1,0:T(8,128)S(1)}, u32[]{:S(2)}, u32[]{:S(2)}) collective-permute-start(f32[16,128]{1,0:T(8,128)S(1)} %get-tuple-element.42), channel_id=1, source_target_pairs={{4,1},{6,3},{8,5},{10,7},{12,9},{14,11},{16,13},{18,15},{20,17},{2... | collective-permute-start | bytes 24584 | tf_op jit(solution)/shard_map/ppermute | solution.py:475
  21.8 3.8 %collective-permute-start = (s32[128]{0:T(128)}, s32[128]{0:T(128)S(1)}, u32[]{:S(2)}, u32[]{:S(2)}) collective-permute-start(s32[128]{0:T(128)} %own_starts.3), channel_id=1, source_target_pairs={{0,2},{1,3},{2,0},{3,1},{4,6},{5,7},{6,4},{7,5},{8,10},{9,11},{10,... | collective-permute-start | bytes 1544 | tf_op jit(solution)/shard_map/ppermute | solution.py:436
  31.9 24.1 %copy-start = (f32[256,512]{1,0:T(8,128)S(1)}, f32[256,512]{1,0:T(8,128)}, u32[]{:S(2)}) copy-start(f32[256,512]{1,0:T(8,128)} %w_ref.1) | copy-start | bytes 1572868
  33.6 1.6 %collective-permute-start.6 = (bf16[272,512]{1,0:T(8,128)(2,1)S(1)}, bf16[272,512]{1,0:T(8,128)(2,1)S(1)}, u32[]{:S(2)}, u32[]{:S(2)}) collective-permute-start(bf16[272,512]{1,0:T(8,128)(2,1)S(1)} %get-tuple-element.50), channel_id=1, source_target_pairs={{0,1},{1,0},{2,3},{3,2},{4,5},{5,4},{6,7},{7,6},{8,9},{9,8},{10,11... | collective-permute-start | bytes 835592 | tf_op jit(solution)/shard_map/ppermute | solution.py:436
  35.3 5.9 %collective-permute-start.7 = (bf16[272,128]{1,0:T(8,128)(2,1)S(1)}, bf16[272,128]{1,0:T(8,128)(2,1)S(1)}, u32[]{:S(2)}, u32[]{:S(2)}) collective-permute-start(bf16[272,128]{1,0:T(8,128)(2,1)S(1)} %get-tuple-element.52), channel_id=1, source_target_pairs={{0,4},{4,0},{8,12},{12,8},{16,20},{20,16},{24,28},{28,24},{1,5},{5... | collective-permute-start | bytes 208904 | tf_op jit(solution)/shard_map/ppermute | solution.py:436
  38.7 5.5 %collective-permute-start.9 = (bf16[256,128]{1,0:T(8,128)(2,1)S(1)}, bf16[256,128]{1,0:T(8,128)(2,1)S(1)}, u32[]{:S(2)}, u32[]{:S(2)}) collective-permute-start(bf16[256,128]{1,0:T(8,128)(2,1)S(1)} %get-tuple-element.54), channel_id=1, source_target_pairs={{0,8},{4,12},{8,0},{12,4},{16,24},{20,28},{24,16},{28,20},{1,9},{5... | collective-permute-start | bytes 196616 | tf_op jit(solution)/shard_map/ppermute | solution.py:436
  41.2 7.4 %collective-permute-start.8 = (bf16[272,128]{1,0:T(8,128)(2,1)S(1)}, bf16[272,128]{1,0:T(8,128)(2,1)S(1)}, u32[]{:S(2)}, u32[]{:S(2)}) collective-permute-start(bf16[272,128]{1,0:T(8,128)(2,1)S(1)} %shard_map.88.a_ref), channel_id=1, source_target_pairs={{0,8},{4,12},{8,0},{12,4},{16,24},{20,28},{24,16},{28,20},{1,9},{5... | collective-permute-start | bytes 208904 | tf_op jit(solution)/shard_map/ppermute | solution.py:436
  44.3 4.3 %collective-permute-start.10 = (bf16[256,128]{1,0:T(8,128)(2,1)S(1)}, bf16[256,128]{1,0:T(8,128)(2,1)S(1)}, u32[]{:S(2)}, u32[]{:S(2)}) collective-permute-start(bf16[256,128]{1,0:T(8,128)(2,1)S(1)} %shard_map.89.b_ref), channel_id=1, source_target_pairs={{0,4},{4,0},{8,12},{12,8},{16,20},{20,16},{24,28},{28,24},{1,5},{5... | collective-permute-start | bytes 196616 | tf_op jit(solution)/shard_map/ppermute | solution.py:436
  48.6 7.4 %collective-permute-start.11 = (bf16[528,128]{1,0:T(8,128)(2,1)S(1)}, bf16[528,128]{1,0:T(8,128)(2,1)S(1)}, u32[]{:S(2)}, u32[]{:S(2)}) collective-permute-start(bf16[528,128]{1,0:T(8,128)(2,1)S(1)} %shard_map.90.mine_ref), channel_id=1, source_target_pairs={{0,16},{4,20},{8,24},{12,28},{16,0},{20,4},{24,8},{28,12},{1,17},{... | collective-permute-start | bytes 405512 | tf_op jit(solution)/shard_map/ppermute | solution.py:436
  56.2 4.4 %collective-permute-start.12 = (bf16[272,128]{1,0:T(8,128)(2,1)S(1)}, bf16[272,128]{1,0:T(8,128)(2,1)S(1)}, u32[]{:S(2)}, u32[]{:S(2)}) collective-permute-start(bf16[272,128]{1,0:T(8,128)(2,1)S(1)} %get-tuple-element.58), channel_id=1, source_target_pairs={{0,4},{4,0},{8,12},{12,8},{16,20},{20,16},{24,28},{28,24},{1,5},{5... | collective-permute-start | bytes 208904 | tf_op jit(solution)/shard_map/ppermute | solution.py:436
  56.9 4.3 %collective-permute-start.13 = (bf16[272,128]{1,0:T(8,128)(2,1)S(1)}, bf16[272,128]{1,0:T(8,128)(2,1)S(1)}, u32[]{:S(2)}, u32[]{:S(2)}) collective-permute-start(bf16[272,128]{1,0:T(8,128)(2,1)S(1)} %get-tuple-element.59), channel_id=1, source_target_pairs={{0,8},{4,12},{8,0},{12,4},{16,24},{20,28},{24,16},{28,20},{1,9},{5... | collective-permute-start | bytes 208904 | tf_op jit(solution)/shard_map/ppermute | solution.py:436
  61.3 9.1 %collective-permute-start.14 = (bf16[1088,128]{1,0:T(8,128)(2,1)S(1)}, bf16[1088,128]{1,0:T(8,128)(2,1)S(1)}, u32[]{:S(2)}, u32[]{:S(2)}) collective-permute-start(bf16[1088,128]{1,0:T(8,128)(2,1)S(1)} %get-tuple-element.61), channel_id=1, source_target_pairs={{0,1},{1,0},{2,3},{3,2},{4,5},{5,4},{6,7},{7,6},{8,9},{9,8},{10,11... | collective-permute-start | bytes 835592 | tf_op jit(solution)/shard_map/ppermute | solution.py:436
  61.3 6.6 %collective-permute-start.15 = (bf16[544,128]{1,0:T(8,128)(2,1)S(1)}, bf16[544,128]{1,0:T(8,128)(2,1)S(1)}, u32[]{:S(2)}, u32[]{:S(2)}) collective-permute-start(bf16[544,128]{1,0:T(8,128)(2,1)S(1)} %get-tuple-element.57.mine_ref), channel_id=1, source_target_pairs={{0,2},{1,3},{2,0},{3,1},{4,6},{5,7},{6,4},{7,5},{8,10},{9,11},{10,... | collective-permute-start | bytes 417800 | tf_op jit(solution)/shard_map/ppermute | solution.py:436
  62.9 7.5 %collective-permute-start.16 = (bf16[544,128]{1,0:T(8,128)(2,1)S(1)}, bf16[544,128]{1,0:T(8,128)(2,1)S(1)}, u32[]{:S(2)}, u32[]{:S(2)}) collective-permute-start(bf16[544,128]{1,0:T(8,128)(2,1)S(1)} %get-tuple-element.60.others_ref), channel_id=1, source_target_pairs={{0,2},{1,3},{2,0},{3,1},{4,6},{5,7},{6,4},{7,5},{8,10},{9,11},{10,... | collective-permute-start | bytes 417800 | tf_op jit(solution)/shard_map/ppermute | solution.py:436
  68.0 3.7 %collective-permute-start.17 = (bf16[544,128]{1,0:T(8,128)(2,1)S(1)}, bf16[544,128]{1,0:T(8,128)(2,1)S(1)}, u32[]{:S(2)}, u32[]{:S(2)}) collective-permute-start(bf16[544,128]{1,0:T(8,128)(2,1)S(1)} %collective-permute-done.15.mine_ref), channel_id=1, source_target_pairs={{0,1},{1,0},{2,3},{3,2},{4,5},{5,4},{6,7},{7,6},{8,9},{9,8},{10,11... | collective-permute-start | bytes 417800 | tf_op jit(solution)/shard_map/ppermute | solution.py:436
  70.4 1.4 %collective-permute-start.18 = (bf16[544,128]{1,0:T(8,128)(2,1)S(1)}, bf16[544,128]{1,0:T(8,128)(2,1)S(1)}, u32[]{:S(2)}, u32[]{:S(2)}) collective-permute-start(bf16[544,128]{1,0:T(8,128)(2,1)S(1)} %collective-permute-done.16.others_ref), channel_id=1, source_target_pairs={{0,1},{1,0},{2,3},{3,2},{4,5},{5,4},{6,7},{7,6},{8,9},{9,8},{10,11... | collective-permute-start | bytes 417800 | tf_op jit(solution)/shard_map/ppermute | solution.py:436
  71.6 21.6 %copy-start.2 = (f32[512,128]{1,0:T(8,128)S(1)}, f32[512,128]{1,0:T(8,128)}, u32[]{:S(2)}) copy-start(f32[512,128]{1,0:T(8,128)} %first_ref.1) | copy-start | bytes 786436
  72.7 1.7 %collective-permute-start.19 = (bf16[272,512]{1,0:T(8,128)(2,1)S(1)}, bf16[272,512]{1,0:T(8,128)(2,1)S(1)}, u32[]{:S(2)}, u32[]{:S(2)}) collective-permute-start(bf16[272,512]{1,0:T(8,128)(2,1)S(1)} %get-tuple-element.69), channel_id=1, source_target_pairs={{0,1},{1,0},{2,3},{3,2},{4,5},{5,4},{6,7},{7,6},{8,9},{9,8},{10,11... | collective-permute-start | bytes 835592 | tf_op jit(solution)/shard_map/ppermute | solution.py:436
  74.4 4.5 %collective-permute-start.20 = (bf16[272,128]{1,0:T(8,128)(2,1)S(1)}, bf16[272,128]{1,0:T(8,128)(2,1)S(1)}, u32[]{:S(2)}, u32[]{:S(2)}) collective-permute-start(bf16[272,128]{1,0:T(8,128)(2,1)S(1)} %get-tuple-element.71), channel_id=1, source_target_pairs={{0,4},{4,0},{8,12},{12,8},{16,20},{20,16},{24,28},{28,24},{1,5},{5... | collective-permute-start | bytes 208904 | tf_op jit(solution)/shard_map/ppermute | solution.py:436
  75.8 4.3 %collective-permute-start.22 = (bf16[256,128]{1,0:T(8,128)(2,1)S(1)}, bf16[256,128]{1,0:T(8,128)(2,1)S(1)}, u32[]{:S(2)}, u32[]{:S(2)}) collective-permute-start(bf16[256,128]{1,0:T(8,128)(2,1)S(1)} %get-tuple-element.73), channel_id=1, source_target_pairs={{0,8},{4,12},{8,0},{12,4},{16,24},{20,28},{24,16},{28,20},{1,9},{5... | collective-permute-start | bytes 196616 | tf_op jit(solution)/shard_map/ppermute | solution.py:436
  78.9 5.5 %collective-permute-start.21 = (bf16[272,128]{1,0:T(8,128)(2,1)S(1)}, bf16[272,128]{1,0:T(8,128)(2,1)S(1)}, u32[]{:S(2)}, u32[]{:S(2)}) collective-permute-start(bf16[272,128]{1,0:T(8,128)(2,1)S(1)} %shard_map.98.a_ref), channel_id=1, source_target_pairs={{0,8},{4,12},{8,0},{12,4},{16,24},{20,28},{24,16},{28,20},{1,9},{5... | collective-permute-start | bytes 208904 | tf_op jit(solution)/shard_map/ppermute | solution.py:436
  80.1 4.3 %collective-permute-start.23 = (bf16[256,128]{1,0:T(8,128)(2,1)S(1)}, bf16[256,128]{1,0:T(8,128)(2,1)S(1)}, u32[]{:S(2)}, u32[]{:S(2)}) collective-permute-start(bf16[256,128]{1,0:T(8,128)(2,1)S(1)} %shard_map.99.b_ref), channel_id=1, source_target_pairs={{0,4},{4,0},{8,12},{12,8},{16,20},{20,16},{24,28},{28,24},{1,5},{5... | collective-permute-start | bytes 196616 | tf_op jit(solution)/shard_map/ppermute | solution.py:436
  84.5 7.6 %collective-permute-start.24 = (bf16[528,128]{1,0:T(8,128)(2,1)S(1)}, bf16[528,128]{1,0:T(8,128)(2,1)S(1)}, u32[]{:S(2)}, u32[]{:S(2)}) collective-permute-start(bf16[528,128]{1,0:T(8,128)(2,1)S(1)} %shard_map.100.mine_ref), channel_id=1, source_target_pairs={{0,16},{4,20},{8,24},{12,28},{16,0},{20,4},{24,8},{28,12},{1,17},{... | collective-permute-start | bytes 405512 | tf_op jit(solution)/shard_map/ppermute | solution.py:436
  87.4 5.8 %collective-permute-start.27 = (f32[256,128]{1,0:T(8,128)S(1)}, f32[256,128]{1,0:T(8,128)S(1)}, u32[]{:S(2)}, u32[]{:S(2)}) collective-permute-start(f32[256,128]{1,0:T(8,128)S(1)} %get-tuple-element.77), channel_id=1, source_target_pairs={{0,1},{1,0},{2,3},{3,2},{4,5},{5,4},{6,7},{7,6},{8,9},{9,8},{10,11... | collective-permute-start | bytes 393224 | tf_op jit(solution)/shard_map/ppermute | solution.py:436
  92.1 5.0 %collective-permute-start.25 = (f32[256,128]{1,0:T(8,128)S(1)}, f32[256,128]{1,0:T(8,128)S(1)}, u32[]{:S(2)}, u32[]{:S(2)}) collective-permute-start(f32[256,128]{1,0:T(8,128)S(1)} %get-tuple-element.74.mine_a), channel_id=1, source_target_pairs={{0,4},{4,0},{8,12},{12,8},{16,20},{20,16},{24,28},{28,24},{1,5},{5... | collective-permute-start | bytes 393224 | tf_op jit(solution)/shard_map/ppermute | solution.py:436
  92.9 5.0 %collective-permute-start.26 = (f32[256,128]{1,0:T(8,128)S(1)}, f32[256,128]{1,0:T(8,128)S(1)}, u32[]{:S(2)}, u32[]{:S(2)}) collective-permute-start(f32[256,128]{1,0:T(8,128)S(1)} %get-tuple-element.75.mine_b), channel_id=1, source_target_pairs={{0,8},{4,12},{8,0},{12,4},{16,24},{20,28},{24,16},{28,20},{1,9},{5... | collective-permute-start | bytes 393224 | tf_op jit(solution)/shard_map/ppermute | solution.py:436
where the time goes:
time: 98.9 us; the launch traced here: 98.8 us
  waiting for transfers between devices  52 us (53%)
  starting transfers between devices  29.8 us (30%)
  Pallas kernels  16 us (16%)
    ppermute x27, waiting for transfers between devices, swap(): lax.ppermute(block, axis, [(i, i ^ bit) for i in range(lax.axis_size(axis...  52 us
    ppermute x27, starting transfers between devices, swap(): lax.ppermute(block, axis, [(i, i ^ bit) for i in range(lax.axis_size(axis...  29.1 us
    pallas_call x28, Pallas kernels, call(): pl.pallas_call(body, out_shape=out_shape, in_specs=in_specs if in_specs i...  16 us
  transfers between devices with their start and end apart: 28, of which 19 were waited for; matrix products, arithmetic and copies ran while one was open for 0% of the time, Pallas kernels for 11%

commit v1 on v0

--- a/solution.py
+++ b/solution.py
@@ -187,7 +187,7 @@
         raw_ref[pl.ds(i, tiles, stride=count), :] = jnp.where(lane < LANES - shift, first, second) * window
         return carry
 
-    lax.fori_loop(0, count, body, 0, unroll=32)
+    lax.fori_loop(0, count, body, 0, unroll=64)
     half = tiles // 2
     for j in range(tiles):
         rows = slice((j // half) * count, (j // half + 1) * count)
@@ -365,43 +365,43 @@
         out_ref[total.shape[0] :, :] = split_stack(aux)
 
 
-def add_chains(a_ref, got_a, b_ref, got_b, out_ref, *, lanes):
-    a, aux = add_blocks(a_ref, got_a, lanes)
-    b, _ = add_blocks(b_ref, got_b, 0)
-    size = b.shape[0]
-    out_ref[0:size, :] = a.astype(BF16)
-    out_ref[size : 2 * size, :] = b.astype(BF16)
-    out_ref[2 * size :, :] = split_stack(aux)
-
-
-def first_templates(w_ref, mine_ref, got_ref, new_a, new_b, send_a, send_b, both_ref):
-    block, width = w_ref.shape
-    rows = block // 4
-    lanes = width // LANES
-    size = lanes * rows
-    numerator, total = add_blocks(mine_ref, got_ref, lanes)
-    for chain, (new, send) in enumerate(((new_a, send_a), (new_b, send_b))):
-        sums = []
-        for lane in range(lanes):
-            old = w_ref[group_rows(chain, True, rows), lane * LANES : (lane + 1) * LANES]
-            at = slice(lane * rows, (lane + 1) * rows)
-            value = old * numerator[chain * size + at.start : chain * size + at.stop] / total[lane : lane + 1, :]
-            new[at, :] = value
-            send[at, :] = value.astype(BF16)
-            sums.append(jnp.sum(value, axis=0, keepdims=True))
-        send[size:, :] = split_stack(jnp.concatenate(sums, axis=0))
-        both_ref[chain * (size + AUX) : (chain + 1) * (size + AUX), :] = send[...]
-
-
-def last_templates(old_a, old_b, mine_ref, got_ref, new_a, new_b, *, lanes):
-    numerator, total = add_blocks(mine_ref, got_ref, lanes)
-    size = old_a.shape[0]
-    rows = size // lanes
-    for chain, (old, new) in enumerate(((old_a, new_a), (old_b, new_b))):
-        for lane in range(lanes):
-            at = slice(lane * rows, (lane + 1) * rows)
-            value = numerator[chain * size + at.start : chain * size + at.stop]
-            new[at, :] = old[at, :] * value / total[lane : lane + 1, :]
+def new_rows(old, mine_ref, got_ref, total_ref, chain, lanes):
+    numerator, total = add_blocks(mine_ref, got_ref, 0 if chain else lanes)
+    if chain:
+        total = total_ref[0:lanes, :]
+    else:
+        total_ref[...] = jnp.zeros_like(total_ref)
+        total_ref[0:lanes, :] = total
+    rows = numerator.shape[0] // lanes
+    for lane in range(lanes):
+        at = slice(lane * rows, (lane + 1) * rows)
+        yield at, old(lane, at) * numerator[at, :] / total[lane : lane + 1, :]
+
+
+def first_templates(w_ref, mine_ref, got_ref, *rest, chain, lanes):
+    total_ref, new, send = rest if chain else rest[::-1]
+    rows = w_ref.shape[0] // 4
+    sums = []
+
+    def old(lane, at):
+        return w_ref[group_rows(chain, True, rows), lane * LANES : (lane + 1) * LANES]
+
+    for at, value in new_rows(old, mine_ref, got_ref, total_ref, chain, lanes):
+        new[at, :] = value
+        send[at, :] = value.astype(BF16)
+        sums.append(jnp.sum(value, axis=0, keepdims=True))
+    send[lanes * rows :, :] = split_stack(jnp.concatenate(sums, axis=0))
+
+
+def last_templates(old_ref, mine_ref, got_ref, *rest, chain, lanes):
+    total_ref, new = rest if chain else rest[::-1]
+    for at, value in new_rows(lambda lane, at: old_ref[at, :], mine_ref, got_ref, total_ref, chain, lanes):
+        new[at, :] = value
+
+
+def join_two(a_ref, b_ref, out_ref):
+    out_ref[0 : a_ref.shape[0], :] = a_ref[...]
+    out_ref[a_ref.shape[0] :, :] = b_ref[...]
 
 
 def join_groups(mine_ref, a_ref, b_ref, others_ref, all_ref):
@@ -536,25 +536,27 @@
         keep_a, keep_b, send_a, send_b = call(
             add_core, (shape(size + AUX, LANES, F32), shape(size, LANES, F32)) + sent, own, total, got,
         )
-        got_a, got_b = swap(send_a, TM, 1), swap(send_b, TM, 2)
-        send_a = call(functools.partial(add_pair, lanes=lanes), sent[0], keep_a, got_a)
-        send_b = call(functools.partial(add_pair, lanes=0), sent[1], keep_b, got_b)
-        got_a, got_b = swap(send_a, TM, 2), swap(send_b, TM, 1)
-        both = shape(2 * size + AUX, LANES, BF16)
-        mine = call(functools.partial(add_chains, lanes=lanes), both, send_a, got_a, send_b, got_b)
-        bit = 4
-        while bit < tm:
-            if bit > 4:
-                mine = call(functools.partial(add_pair, lanes=lanes), both, mine, got)
-            got = swap(mine, TM, bit)
-            bit *= 2
+        sides = []
+        for keep, send, bits in ((keep_a, send_a, (1, 2)), (keep_b, send_b, (2, 1))):
+            sides.append([keep, swap(send, TM, bits[0])])
+        for chain, bits in enumerate(((1, 2), (2, 1))):
+            aux = 0 if chain else lanes
+            for bit in (bits[1],) + tuple(4 << i for i in range((tm // 4).bit_length() - 1)):
+                mine = call(functools.partial(add_pair, lanes=aux), sent[chain], *sides[chain])
+                sides[chain] = [mine, swap(mine, TM, bit)]
         part = shape(size, LANES, F32)
+        totals = shape(8, LANES, F32)
         if iteration < ITERS - 1:
-            kept_a, kept_b, send_a, send_b, pieces = call(
-                first_templates,
-                (part, part, sent[0], sent[0], shape(2 * (size + AUX), LANES, BF16)), templates, mine, got,
-            )
-            other_a, other_b = swap(send_a, TM, 1), swap(send_b, TM, 2)
+            send_a, kept_a, total = call(
+                functools.partial(first_templates, chain=0, lanes=lanes), (sent[0], part, totals), templates, *sides[0],
+            )
+            other_a = swap(send_a, TM, 1)
+            kept_b, send_b = call(
+                functools.partial(first_templates, chain=1, lanes=lanes), (part, sent[0]), templates, *sides[1],
+                total,
+            )
+            other_b = swap(send_b, TM, 2)
+            pieces = call(join_two, shape(2 * (size + AUX), LANES, BF16), send_a, send_b)
             pair = shape(2 * (size + AUX), LANES, BF16), shape(4 * (size + AUX), LANES, BF16)
             others, both_groups = call(join_groups, pair, pieces, other_a, other_b)
             in_y = [swap(pieces, FREQ, 2)]
@@ -564,10 +566,13 @@
             pieces.append(swap(in_y[0], FREQ, 1))
             pieces.append(swap(in_y[1], FREQ, 1))
         else:
-            new_a, new_b = call(
-                functools.partial(last_templates, lanes=lanes), (part, part), kept_a, kept_b, mine, got,
+            new_a, total = call(
+                functools.partial(last_templates, chain=0, lanes=lanes), (part, totals), kept_a, *sides[0],
             )
             other_a = swap(new_a, TM, 1)
+            new_b = call(
+                functools.partial(last_templates, chain=1, lanes=lanes), part, kept_b, *sides[1], total,
+            )
             other_b = swap(new_b, TM, 2)
             acts = call(
                 place_acts, shape(2 * count, quarter, F32), keep_acts, given, activations,

time: 98.9 us -> 97 us (0.981)
  waiting for transfers between devices: 52 us -> 47 us
  starting transfers between devices: 29.8 us -> 33 us
    ppermute x27 -> x29, waiting for transfers between devices: 52 us -> 47 us  [swap(): lax.ppermute(block, axis, [(i, i ^ bit) for i in range(lax.axis_size(axis...]
    ppermute x27 -> x29, starting transfers between devices: 29.1 us -> 32.4 us  [swap(): lax.ppermute(block, axis, [(i, i ^ bit) for i in range(lax.axis_size(axis...]
    pallas_call x28 -> x33, Pallas kernels: 16 us -> 15.9 us  [call(): pl.pallas_call(body, out_shape=out_shape, in_specs=in_specs if in_specs i...]
  transfers between devices with their start and end apart: 28 -> 30, of which waited for: 19 -> 21; matrix products, arithmetic and copies ran while one was open for 0% -> 0% of each run, Pallas kernels for 11% -> 11%
where the time goes in v1:
time: 97 us; the launch traced here: 96.8 us
  waiting for transfers between devices  47 us (48%)
  starting transfers between devices  33 us (34%)
  Pallas kernels  15.9 us (16%)
    ppermute x29, waiting for transfers between devices, swap(): lax.ppermute(block, axis, [(i, i ^ bit) for i in range(lax.axis_size(axis...  47 us
    ppermute x29, starting transfers between devices, swap(): lax.ppermute(block, axis, [(i, i ^ bit) for i in range(lax.axis_size(axis...  32.4 us
    pallas_call x33, Pallas kernels, call(): pl.pallas_call(body, out_shape=out_shape, in_specs=in_specs if in_specs i...  15.9 us
  transfers between devices with their start and end apart: 30, of which 21 were waited for; matrix products, arithmetic and copies ran while one was open for 0% of the time, Pallas kernels for 11%

profile of v1, /device:TPU:0, one launch (start us, length us, event | category | flops | bytes accessed | tf_op | source)
XLA Modules:
  0.0 96.8 jit_solution(12762893307344623608)
XLA Ops:
  0.7 1.5 %shard_map.77 = (bf16[272,768]{1,0:T(8,128)(2,1)S(1)}, f32[128,1024]{1,0:T(8,128)S(1)}, f32[16,128]{1,0:T(8,128)S(1)}) custom-call(f32[256,512]{1,0:T(8,128)} %w_ref.3, f32[512,128]{1,0:T(8,128)} %first_ref.1, f32[128,1024]{1,0:T(8,128)} %constant.4.clone.base_hbm, f32[256,128]{1,0:T(8,128)} %bitcast.1), custom_call_target="tpu_custom_call" | custom-call | bytes 1048576 | tf_op jit(solution)/shard_map/pallas_call | solution.py:60
  2.1 3.1 %collective-permute-start.4 = (bf16[272,768]{1,0:T(8,128)(2,1)S(1)}, bf16[272,768]{1,0:T(8,128)(2,1)S(1)}, u32[]{:S(2)}, u32[]{:S(2)}) collective-permute-start(bf16[272,768]{1,0:T(8,128)(2,1)S(1)} %get-tuple-element.46.own_ref.own_pack), channel_id=1, source_target_pairs={{0,2},{1,3},{2,0},{3,1},{4,6},{5,7},{6,4},{7,5},{8,10},{9,11},{10,... | collective-permute-start | bytes 1253384 | tf_op jit(solution)/shard_map/ppermute | solution.py:436
  5.2 9.6 %collective-permute-done.4.side_ref.side_pack = bf16[272,768]{1,0:T(8,128)(2,1)S(1)} collective-permute-done((bf16[272,768]{1,0:T(8,128)(2,1)S(1)}, bf16[272,768]{1,0:T(8,128)(2,1)S(1)}, u32[]{:S(2)}, u32[]{:S(2)}) %collective-permute-start.4) | collective-permute-done | bytes 417824 | tf_op jit(solution)/shard_map/ppermute | solution.py:436
  14.8 0.1 shard_map.84
  14.9 0.1 collective-permute-start.5
  15.0 1.8 %collective-permute-start.1 = (f32[256,128]{1,0:T(8,128)}, f32[256,128]{1,0:T(8,128)S(1)}, u32[]{:S(2)}, u32[]{:S(2)}) collective-permute-start(f32[256,128]{1,0:T(8,128)} %bitcast.2), channel_id=1, source_target_pairs={{0,2},{1,3},{2,0},{3,1},{4,6},{5,7},{6,4},{7,5},{8,10},{9,11},{10,... | collective-permute-start | bytes 393224 | tf_op jit(solution)/shard_map/ppermute | solution.py:436
  16.8 4.3 %collective-permute-done.1.side_ref.side_wave = f32[256,128]{1,0:T(8,128)S(1)} collective-permute-done((f32[256,128]{1,0:T(8,128)}, f32[256,128]{1,0:T(8,128)S(1)}, u32[]{:S(2)}, u32[]{:S(2)}) %collective-permute-start.1) | collective-permute-done | bytes 131104 | tf_op jit(solution)/shard_map/ppermute | solution.py:436
  21.1 0.7 collective-permute-start.3
  21.8 1.8 %collective-permute-start = (s32[128]{0:T(128)}, s32[128]{0:T(128)S(1)}, u32[]{:S(2)}, u32[]{:S(2)}) collective-permute-start(s32[128]{0:T(128)} %own_starts.3), channel_id=1, source_target_pairs={{0,2},{1,3},{2,0},{3,1},{4,6},{5,7},{6,4},{7,5},{8,10},{9,11},{10,... | collective-permute-start | bytes 1544 | tf_op jit(solution)/shard_map/ppermute | solution.py:436
  23.6 1.3 %shard_map.81.table_ref = bf16[1024,2048]{1,0:T(8,128)(2,1)S(1)} custom-call(f32[128,1024]{1,0:T(8,128)S(1)} %get-tuple-element.43.base_ref), custom_call_target="tpu_custom_call" | custom-call | flops 4194304 | bytes 8388608 | tf_op jit(solution)/shard_map/pallas_call | solution.py:60
  24.9 0.7 collective-permute-done.side_starts
  25.6 1.8 %shard_map.79.front_ref = bf16[256,1024]{1,0:T(8,128)(2,1)S(1)} custom-call(s32[128]{0:T(128)S(1)} %copy-done.4, s32[128]{0:T(128)S(1)} %collective-permute-done.side_starts, f32[256,128]{1,0:T(8,128)S(1)} %bitcast.3, f32[256,128]{1,0:T(8,128)S(1)} %collective-permute-done.1.side_ref.side_wave, f32[32,128]{1,0:T(8,128)S(1)} %collective-permute-done.2.heads_ref, ...), custom_call_target="tpu_custom_call" | custom-call | bytes 4194304 | tf_op jit(solution)/shard_map/pallas_call | solution.py:60
  27.4 1.8 %shard_map.80.back_ref = bf16[256,1024]{1,0:T(8,128)(2,1)S(1)} custom-call(s32[128]{0:T(128)S(1)} %copy-done.4, s32[128]{0:T(128)S(1)} %collective-permute-done.side_starts, f32[256,128]{1,0:T(8,128)S(1)} %bitcast.4, f32[256,128]{1,0:T(8,128)S(1)} %collective-permute-done.1.side_ref.side_wave, f32[32,128]{1,0:T(8,128)S(1)} %collective-permute-done.2.heads_ref, ...), custom_call_target="tpu_custom_call" | custom-call | bytes 4194304 | tf_op jit(solution)/shard_map/pallas_call | solution.py:60
  29.2 1.3 %shard_map.82 = (f32[256,512]{1,0:T(8,128)S(1)}, f32[512,256]{1,0:T(8,128)S(1)}) custom-call(bf16[256,1024]{1,0:T(8,128)(2,1)S(1)} %shard_map.79.front_ref, bf16[256,1024]{1,0:T(8,128)(2,1)S(1)} %shard_map.80.back_ref, bf16[1024,2048]{1,0:T(8,128)(2,1)S(1)} %shard_map.81.table_ref), custom_call_target="tpu_custom_call" | custom-call | flops 1073741824 | bytes 8388608 | tf_op jit(solution)/shard_map/pallas_call | solution.py:60
  30.5 1.3 %shard_map.83.later_ref.energy_ref = f32[256,512]{1,0:T(8,128)S(1)} custom-call(bf16[256,1024]{1,0:T(8,128)(2,1)S(1)} %shard_map.79.front_ref, bf16[256,1024]{1,0:T(8,128)(2,1)S(1)} %shard_map.80.back_ref, bf16[1024,2048]{1,0:T(8,128)(2,1)S(1)} %shard_map.81.table_ref), custom_call_target="tpu_custom_call" | custom-call | flops 1073741824 | bytes 8388608 | tf_op jit(solution)/shard_map/pallas_call | solution.py:60
  31.8 1.6 %shard_map.85 = (bf16[272,512]{1,0:T(8,128)(2,1)S(1)}, f32[256,512]{1,0:T(8,128)S(1)}, f32[8,512]{1,0:T(8,128)S(1)}, bf16[256,512]{1,0:T(8,128)(2,1)S(1)}) custom-call(f32[256,512]{1,0:T(8,128)S(1)} %get-tuple-element.44.energy_ref, f32[256,512]{1,0:T(8,128)S(1)} %shard_map.83.later_ref.energy_ref, f32[512,256]{1,0:T(8,128)S(1)} %get-tuple-element.45.turned_ref, ...), custom_call_target="tpu_custom_call" | custom-call | flops 805306368 | bytes 4194304 | tf_op jit(solution)/shard_map/pallas_call | solution.py:60
  33.4 0.3 collective-permute-start.6
  33.7 0.5 shard_map.86.own_ref
  34.2 0.9 collective-permute-done.6.got_ref
  35.1 0.1 shard_map.87
  35.1 3.4 %collective-permute-start.7 = (bf16[272,128]{1,0:T(8,128)(2,1)S(1)}, bf16[272,128]{1,0:T(8,128)(2,1)S(1)}, u32[]{:S(2)}, u32[]{:S(2)}) collective-permute-start(bf16[272,128]{1,0:T(8,128)(2,1)S(1)} %get-tuple-element.52), channel_id=1, source_target_pairs={{0,4},{4,0},{8,12},{12,8},{16,20},{20,16},{24,28},{28,24},{1,5},{5... | collective-permute-start | bytes 208904 | tf_op jit(solution)/shard_map/ppermute | solution.py:436
  38.6 1.8 %collective-permute-start.10 = (bf16[256,128]{1,0:T(8,128)(2,1)S(1)}, bf16[256,128]{1,0:T(8,128)(2,1)S(1)}, u32[]{:S(2)}, u32[]{:S(2)}) collective-permute-start(bf16[256,128]{1,0:T(8,128)(2,1)S(1)} %get-tuple-element.56), channel_id=1, source_target_pairs={{0,8},{4,12},{8,0},{12,4},{16,24},{20,28},{24,16},{28,20},{1,9},{5... | collective-permute-start | bytes 196616 | tf_op jit(solution)/shard_map/ppermute | solution.py:436
  40.4 0.7 collective-permute-done.7.got_ref
  41.1 3.0 %collective-permute-start.8 = (bf16[272,128]{1,0:T(8,128)(2,1)S(1)}, bf16[272,128]{1,0:T(8,128)(2,1)S(1)}, u32[]{:S(2)}, u32[]{:S(2)}) collective-permute-start(bf16[272,128]{1,0:T(8,128)(2,1)S(1)} %shard_map.88.mine_ref), channel_id=1, source_target_pairs={{0,8},{4,12},{8,0},{12,4},{16,24},{20,28},{24,16},{28,20},{1,9},{5... | collective-permute-start | bytes 208904 | tf_op jit(solution)/shard_map/ppermute | solution.py:436
  44.1 0.7 collective-permute-start.11
  44.9 1.5 %collective-permute-done.8.got_ref = bf16[272,128]{1,0:T(8,128)(2,1)S(1)} collective-permute-done((bf16[272,128]{1,0:T(8,128)(2,1)S(1)}, bf16[272,128]{1,0:T(8,128)(2,1)S(1)}, u32[]{:S(2)}, u32[]{:S(2)}) %collective-permute-start.8) | collective-permute-done | bytes 69664 | tf_op jit(solution)/shard_map/ppermute | solution.py:436
  46.4 3.1 %collective-permute-start.9 = (bf16[272,128]{1,0:T(8,128)(2,1)S(1)}, bf16[272,128]{1,0:T(8,128)(2,1)S(1)}, u32[]{:S(2)}, u32[]{:S(2)}) collective-permute-start(bf16[272,128]{1,0:T(8,128)(2,1)S(1)} %shard_map.89.mine_ref), channel_id=1, source_target_pairs={{0,16},{4,20},{8,24},{12,28},{16,0},{20,4},{24,8},{28,12},{1,17},{... | collective-permute-start | bytes 208904 | tf_op jit(solution)/shard_map/ppermute | solution.py:436
  49.6 1.6 %collective-permute-start.12 = (bf16[256,128]{1,0:T(8,128)(2,1)S(1)}, bf16[256,128]{1,0:T(8,128)(2,1)S(1)}, u32[]{:S(2)}, u32[]{:S(2)}) collective-permute-start(bf16[256,128]{1,0:T(8,128)(2,1)S(1)} %shard_map.92.mine_ref), channel_id=1, source_target_pairs={{0,16},{4,20},{8,24},{12,28},{16,0},{20,4},{24,8},{28,12},{1,17},{... | collective-permute-start | bytes 196616 | tf_op jit(solution)/shard_map/ppermute | solution.py:436
  51.2 2.4 %collective-permute-done.9.got_ref = bf16[272,128]{1,0:T(8,128)(2,1)S(1)} collective-permute-done((bf16[272,128]{1,0:T(8,128)(2,1)S(1)}, bf16[272,128]{1,0:T(8,128)(2,1)S(1)}, u32[]{:S(2)}, u32[]{:S(2)}) %collective-permute-start.9) | collective-permute-done | bytes 69664 | tf_op jit(solution)/shard_map/ppermute | solution.py:436
  53.6 1.2 %collective-permute-done.12.got_ref = bf16[256,128]{1,0:T(8,128)(2,1)S(1)} collective-permute-done((bf16[256,128]{1,0:T(8,128)(2,1)S(1)}, bf16[256,128]{1,0:T(8,128)(2,1)S(1)}, u32[]{:S(2)}, u32[]{:S(2)}) %collective-permute-start.12) | collective-permute-done | bytes 65568 | tf_op jit(solution)/shard_map/ppermute | solution.py:436
  54.9 2.0 %collective-permute-start.14 = (bf16[272,128]{1,0:T(8,128)(2,1)S(1)}, bf16[272,128]{1,0:T(8,128)(2,1)S(1)}, u32[]{:S(2)}, u32[]{:S(2)}) collective-permute-start(bf16[272,128]{1,0:T(8,128)(2,1)S(1)} %get-tuple-element.58.b_ref), channel_id=1, source_target_pairs={{0,8},{4,12},{8,0},{12,4},{16,24},{20,28},{24,16},{28,20},{1,9},{5... | collective-permute-start | bytes 208904 | tf_op jit(solution)/shard_map/ppermute | solution.py:436
  56.8 0.6 collective-permute-start.13
  57.5 1.8 %collective-permute-done.14.b_ref = bf16[272,128]{1,0:T(8,128)(2,1)S(1)} collective-permute-done((bf16[272,128]{1,0:T(8,128)(2,1)S(1)}, bf16[272,128]{1,0:T(8,128)(2,1)S(1)}, u32[]{:S(2)}, u32[]{:S(2)}) %collective-permute-start.14) | collective-permute-done | bytes 69664 | tf_op jit(solution)/shard_map/ppermute | solution.py:436
  59.2 1.9 %collective-permute-done.13.a_ref = bf16[272,128]{1,0:T(8,128)(2,1)S(1)} collective-permute-done((bf16[272,128]{1,0:T(8,128)(2,1)S(1)}, bf16[272,128]{1,0:T(8,128)(2,1)S(1)}, u32[]{:S(2)}, u32[]{:S(2)}) %collective-permute-start.13) | collective-permute-done | bytes 69664 | tf_op jit(solution)/shard_map/ppermute | solution.py:436
  61.2 0.1 collective-permute-start.15
  61.3 1.6 %collective-permute-start.16 = (bf16[544,128]{1,0:T(8,128)(2,1)S(1)}, bf16[544,128]{1,0:T(8,128)(2,1)S(1)}, u32[]{:S(2)}, u32[]{:S(2)}) collective-permute-start(bf16[544,128]{1,0:T(8,128)(2,1)S(1)} %shard_map.94.mine_ref), channel_id=1, source_target_pairs={{0,2},{1,3},{2,0},{3,1},{4,6},{5,7},{6,4},{7,5},{8,10},{9,11},{10,... | collective-permute-start | bytes 417800 | tf_op jit(solution)/shard_map/ppermute | solution.py:436
  62.9 0.5 collective-permute-start.17
  63.4 4.5 %collective-permute-done.16.mine_ref = bf16[544,128]{1,0:T(8,128)(2,1)S(1)} collective-permute-done((bf16[544,128]{1,0:T(8,128)(2,1)S(1)}, bf16[544,128]{1,0:T(8,128)(2,1)S(1)}, u32[]{:S(2)}, u32[]{:S(2)}) %collective-permute-start.16) | collective-permute-done | bytes 139296 | tf_op jit(solution)/shard_map/ppermute | solution.py:436
  67.9 2.4 %collective-permute-done.17.others_ref = bf16[544,128]{1,0:T(8,128)(2,1)S(1)} collective-permute-done((bf16[544,128]{1,0:T(8,128)(2,1)S(1)}, bf16[544,128]{1,0:T(8,128)(2,1)S(1)}, u32[]{:S(2)}, u32[]{:S(2)}) %collective-permute-start.17) | collective-permute-done | bytes 139296 | tf_op jit(solution)/shard_map/ppermute | solution.py:436
  70.3 0.6 shard_map.96
  71.0 0.5 shard_map.97
  71.6 0.1 collective-permute-done.19.others_ref
  71.7 0.9 shard_map.98
  72.6 0.5 collective-permute-start.20
  73.1 0.5 shard_map.99.own_ref
  73.6 0.7 collective-permute-done.20.got_ref
  74.3 0.7 collective-permute-start.21
  75.0 0.1 collective-permute-start.24
  75.2 3.7 %collective-permute-done.21.got_ref = bf16[272,128]{1,0:T(8,128)(2,1)S(1)} collective-permute-done((bf16[272,128]{1,0:T(8,128)(2,1)S(1)}, bf16[272,128]{1,0:T(8,128)(2,1)S(1)}, u32[]{:S(2)}, u32[]{:S(2)}) %collective-permute-start.21) | collective-permute-done | bytes 69664 | tf_op jit(solution)/shard_map/ppermute | solution.py:436
  78.9 0.2 collective-permute-start.22
  79.1 0.2 collective-permute-done.24.got_ref
  79.3 1.5 %collective-permute-start.25 = (bf16[256,128]{1,0:T(8,128)(2,1)S(1)}, bf16[256,128]{1,0:T(8,128)(2,1)S(1)}, u32[]{:S(2)}, u32[]{:S(2)}) collective-permute-start(bf16[256,128]{1,0:T(8,128)(2,1)S(1)} %shard_map.104.mine_ref), channel_id=1, source_target_pairs={{0,4},{4,0},{8,12},{12,8},{16,20},{20,16},{24,28},{28,24},{1,5},{5... | collective-permute-start | bytes 196616 | tf_op jit(solution)/shard_map/ppermute | solution.py:436
  80.8 2.5 %collective-permute-done.22.got_ref = bf16[272,128]{1,0:T(8,128)(2,1)S(1)} collective-permute-done((bf16[272,128]{1,0:T(8,128)(2,1)S(1)}, bf16[272,128]{1,0:T(8,128)(2,1)S(1)}, u32[]{:S(2)}, u32[]{:S(2)}) %collective-permute-start.22) | collective-permute-done | bytes 69664 | tf_op jit(solution)/shard_map/ppermute | solution.py:436
  83.3 1.8 %collective-permute-start.23 = (bf16[272,128]{1,0:T(8,128)(2,1)S(1)}, bf16[272,128]{1,0:T(8,128)(2,1)S(1)}, u32[]{:S(2)}, u32[]{:S(2)}) collective-permute-start(bf16[272,128]{1,0:T(8,128)(2,1)S(1)} %shard_map.102.mine_ref), channel_id=1, source_target_pairs={{0,16},{4,20},{8,24},{12,28},{16,0},{20,4},{24,8},{28,12},{1,17},{... | collective-permute-start | bytes 208904 | tf_op jit(solution)/shard_map/ppermute | solution.py:436
  85.1 1.2 %collective-permute-start.26 = (bf16[256,128]{1,0:T(8,128)(2,1)S(1)}, bf16[256,128]{1,0:T(8,128)(2,1)S(1)}, u32[]{:S(2)}, u32[]{:S(2)}) collective-permute-start(bf16[256,128]{1,0:T(8,128)(2,1)S(1)} %shard_map.105.mine_ref), channel_id=1, source_target_pairs={{0,16},{4,20},{8,24},{12,28},{16,0},{20,4},{24,8},{28,12},{1,17},{... | collective-permute-start | bytes 196616 | tf_op jit(solution)/shard_map/ppermute | solution.py:436
  86.4 0.1 collective-permute-start.29
  86.5 2.9 %collective-permute-done.23.got_ref = bf16[272,128]{1,0:T(8,128)(2,1)S(1)} collective-permute-done((bf16[272,128]{1,0:T(8,128)(2,1)S(1)}, bf16[272,128]{1,0:T(8,128)(2,1)S(1)}, u32[]{:S(2)}, u32[]{:S(2)}) %collective-permute-start.23) | collective-permute-done | bytes 69664 | tf_op jit(solution)/shard_map/ppermute | solution.py:436
  89.5 1.4 %collective-permute-done.26.got_ref = bf16[256,128]{1,0:T(8,128)(2,1)S(1)} collective-permute-done((bf16[256,128]{1,0:T(8,128)(2,1)S(1)}, bf16[256,128]{1,0:T(8,128)(2,1)S(1)}, u32[]{:S(2)}, u32[]{:S(2)}) %collective-permute-start.26) | collective-permute-done | bytes 65568 | tf_op jit(solution)/shard_map/ppermute | solution.py:436
  90.9 0.1 collective-permute-start.28
  90.9 0.7 collective-permute-start.27
  91.7 0.8 shard_map.109
  92.4 3.5 %collective-permute-done.28.got_b = f32[256,128]{1,0:T(8,128)S(1)} collective-permute-done((f32[256,128]{1,0:T(8,128)S(1)}, f32[256,128]{1,0:T(8,128)S(1)}, u32[]{:S(2)}, u32[]{:S(2)}) %collective-permute-start.28) | collective-permute-done | bytes 131104 | tf_op jit(solution)/shard_map/ppermute | solution.py:436
  95.9 0.1 collective-permute-done.27.got_a
  96.0 0.8 shard_map.107
  (39 shorter events, 0.6 us)
Async XLA Ops:
  0.6 24.9 %copy-start.3 = (f32[16,128]{1,0:T(8,128)S(1)}, f32[16,128]{1,0:T(8,128)}, u32[]{:S(2)}) copy-start(f32[16,128]{1,0:T(8,128)} %constant.5.clone.rest_0_.rest_1_) | copy-start | bytes 24580
  0.6 24.9 %copy-start.1 = (f32[32768]{0:T(1024)S(1)}, f32[32768]{0:T(1024)}, u32[]{:S(2)}) copy-start(f32[32768]{0:T(1024)} %param.6) | copy-start | bytes 393220
  0.7 24.9 %copy-start.4 = (s32[128]{0:T(128)S(1)}, s32[128]{0:T(128)}, u32[]{:S(2)}) copy-start(s32[128]{0:T(128)} %own_starts.3) | copy-start | bytes 1540
  2.1 12.7 %collective-permute-start.4 = (bf16[272,768]{1,0:T(8,128)(2,1)S(1)}, bf16[272,768]{1,0:T(8,128)(2,1)S(1)}, u32[]{:S(2)}, u32[]{:S(2)}) collective-permute-start(bf16[272,768]{1,0:T(8,128)(2,1)S(1)} %get-tuple-element.46.own_ref.own_pack), channel_id=1, source_target_pairs={{0,2},{1,3},{2,0},{3,1},{4,6},{5,7},{6,4},{7,5},{8,10},{9,11},{10,... | collective-permute-start | bytes 1253384 | tf_op jit(solution)/shard_map/ppermute | solution.py:436
  14.9 16.9 %collective-permute-start.5 = (bf16[544,640]{1,0:T(8,128)(2,1)S(1)}, bf16[544,640]{1,0:T(8,128)(2,1)S(1)}, u32[]{:S(2)}, u32[]{:S(2)}) collective-permute-start(bf16[544,640]{1,0:T(8,128)(2,1)S(1)} %shard_map.84), channel_id=1, source_target_pairs={{0,1},{1,0},{2,3},{3,2},{4,5},{5,4},{6,7},{7,6},{8,9},{9,8},{10,11... | collective-permute-start | bytes 2088968 | tf_op jit(solution)/shard_map/ppermute | solution.py:436
  15.0 6.1 %collective-permute-start.1 = (f32[256,128]{1,0:T(8,128)}, f32[256,128]{1,0:T(8,128)S(1)}, u32[]{:S(2)}, u32[]{:S(2)}) collective-permute-start(f32[256,128]{1,0:T(8,128)} %bitcast.2), channel_id=1, source_target_pairs={{0,2},{1,3},{2,0},{3,1},{4,6},{5,7},{6,4},{7,5},{8,10},{9,11},{10,... | collective-permute-start | bytes 393224 | tf_op jit(solution)/shard_map/ppermute | solution.py:436
  21.1 4.4 %collective-permute-start.2 = (f32[32,128]{1,0:T(8,128)S(1)}, f32[32,128]{1,0:T(8,128)S(1)}, u32[]{:S(2)}, u32[]{:S(2)}) collective-permute-start(f32[32,128]{1,0:T(8,128)S(1)} %get-tuple-element.41), channel_id=1, source_target_pairs={{0,1},{1,0},{2,3},{3,2},{4,5},{5,4},{6,7},{7,6},{8,9},{9,8},{10,11... | collective-permute-start | bytes 49160 | tf_op jit(solution)/shard_map/ppermute | solution.py:436
  21.1 6.3 %collective-permute-start.3 = (f32[16,128]{1,0:T(8,128)S(1)}, f32[16,128]{1,0:T(8,128)S(1)}, u32[]{:S(2)}, u32[]{:S(2)}) collective-permute-start(f32[16,128]{1,0:T(8,128)S(1)} %get-tuple-element.42), channel_id=1, source_target_pairs={{4,1},{6,3},{8,5},{10,7},{12,9},{14,11},{16,13},{18,15},{20,17},{2... | collective-permute-start | bytes 24584 | tf_op jit(solution)/shard_map/ppermute | solution.py:475
  21.8 3.8 %collective-permute-start = (s32[128]{0:T(128)}, s32[128]{0:T(128)S(1)}, u32[]{:S(2)}, u32[]{:S(2)}) collective-permute-start(s32[128]{0:T(128)} %own_starts.3), channel_id=1, source_target_pairs={{0,2},{1,3},{2,0},{3,1},{4,6},{5,7},{6,4},{7,5},{8,10},{9,11},{10,... | collective-permute-start | bytes 1544 | tf_op jit(solution)/shard_map/ppermute | solution.py:436
  31.8 21.8 %copy-start = (f32[256,512]{1,0:T(8,128)S(1)}, f32[256,512]{1,0:T(8,128)}, u32[]{:S(2)}) copy-start(f32[256,512]{1,0:T(8,128)} %w_ref.3) | copy-start | bytes 1572868
  33.4 1.6 %collective-permute-start.6 = (bf16[272,512]{1,0:T(8,128)(2,1)S(1)}, bf16[272,512]{1,0:T(8,128)(2,1)S(1)}, u32[]{:S(2)}, u32[]{:S(2)}) collective-permute-start(bf16[272,512]{1,0:T(8,128)(2,1)S(1)} %get-tuple-element.50), channel_id=1, source_target_pairs={{0,1},{1,0},{2,3},{3,2},{4,5},{5,4},{6,7},{7,6},{8,9},{9,8},{10,11... | collective-permute-start | bytes 835592 | tf_op jit(solution)/shard_map/ppermute | solution.py:436
  35.1 5.9 %collective-permute-start.7 = (bf16[272,128]{1,0:T(8,128)(2,1)S(1)}, bf16[272,128]{1,0:T(8,128)(2,1)S(1)}, u32[]{:S(2)}, u32[]{:S(2)}) collective-permute-start(bf16[272,128]{1,0:T(8,128)(2,1)S(1)} %get-tuple-element.52), channel_id=1, source_target_pairs={{0,4},{4,0},{8,12},{12,8},{16,20},{20,16},{24,28},{28,24},{1,5},{5... | collective-permute-start | bytes 208904 | tf_op jit(solution)/shard_map/ppermute | solution.py:436
  38.6 5.5 %collective-permute-start.10 = (bf16[256,128]{1,0:T(8,128)(2,1)S(1)}, bf16[256,128]{1,0:T(8,128)(2,1)S(1)}, u32[]{:S(2)}, u32[]{:S(2)}) collective-permute-start(bf16[256,128]{1,0:T(8,128)(2,1)S(1)} %get-tuple-element.56), channel_id=1, source_target_pairs={{0,8},{4,12},{8,0},{12,4},{16,24},{20,28},{24,16},{28,20},{1,9},{5... | collective-permute-start | bytes 196616 | tf_op jit(solution)/shard_map/ppermute | solution.py:436
  41.1 5.3 %collective-permute-start.8 = (bf16[272,128]{1,0:T(8,128)(2,1)S(1)}, bf16[272,128]{1,0:T(8,128)(2,1)S(1)}, u32[]{:S(2)}, u32[]{:S(2)}) collective-permute-start(bf16[272,128]{1,0:T(8,128)(2,1)S(1)} %shard_map.88.mine_ref), channel_id=1, source_target_pairs={{0,8},{4,12},{8,0},{12,4},{16,24},{20,28},{24,16},{28,20},{1,9},{5... | collective-permute-start | bytes 208904 | tf_op jit(solution)/shard_map/ppermute | solution.py:436
  44.1 5.4 %collective-permute-start.11 = (bf16[256,128]{1,0:T(8,128)(2,1)S(1)}, bf16[256,128]{1,0:T(8,128)(2,1)S(1)}, u32[]{:S(2)}, u32[]{:S(2)}) collective-permute-start(bf16[256,128]{1,0:T(8,128)(2,1)S(1)} %shard_map.91.mine_ref), channel_id=1, source_target_pairs={{0,4},{4,0},{8,12},{12,8},{16,20},{20,16},{24,28},{28,24},{1,5},{5... | collective-permute-start | bytes 196616 | tf_op jit(solution)/shard_map/ppermute | solution.py:436
  46.4 7.1 %collective-permute-start.9 = (bf16[272,128]{1,0:T(8,128)(2,1)S(1)}, bf16[272,128]{1,0:T(8,128)(2,1)S(1)}, u32[]{:S(2)}, u32[]{:S(2)}) collective-permute-start(bf16[272,128]{1,0:T(8,128)(2,1)S(1)} %shard_map.89.mine_ref), channel_id=1, source_target_pairs={{0,16},{4,20},{8,24},{12,28},{16,0},{20,4},{24,8},{28,12},{1,17},{... | collective-permute-start | bytes 208904 | tf_op jit(solution)/shard_map/ppermute | solution.py:436
  49.6 5.3 %collective-permute-start.12 = (bf16[256,128]{1,0:T(8,128)(2,1)S(1)}, bf16[256,128]{1,0:T(8,128)(2,1)S(1)}, u32[]{:S(2)}, u32[]{:S(2)}) collective-permute-start(bf16[256,128]{1,0:T(8,128)(2,1)S(1)} %shard_map.92.mine_ref), channel_id=1, source_target_pairs={{0,16},{4,20},{8,24},{12,28},{16,0},{20,4},{24,8},{28,12},{1,17},{... | collective-permute-start | bytes 196616 | tf_op jit(solution)/shard_map/ppermute | solution.py:436
  54.9 4.4 %collective-permute-start.14 = (bf16[272,128]{1,0:T(8,128)(2,1)S(1)}, bf16[272,128]{1,0:T(8,128)(2,1)S(1)}, u32[]{:S(2)}, u32[]{:S(2)}) collective-permute-start(bf16[272,128]{1,0:T(8,128)(2,1)S(1)} %get-tuple-element.58.b_ref), channel_id=1, source_target_pairs={{0,8},{4,12},{8,0},{12,4},{16,24},{20,28},{24,16},{28,20},{1,9},{5... | collective-permute-start | bytes 208904 | tf_op jit(solution)/shard_map/ppermute | solution.py:436
  56.8 4.3 %collective-permute-start.13 = (bf16[272,128]{1,0:T(8,128)(2,1)S(1)}, bf16[272,128]{1,0:T(8,128)(2,1)S(1)}, u32[]{:S(2)}, u32[]{:S(2)}) collective-permute-start(bf16[272,128]{1,0:T(8,128)(2,1)S(1)} %get-tuple-element.54.a_ref), channel_id=1, source_target_pairs={{0,4},{4,0},{8,12},{12,8},{16,20},{20,16},{24,28},{28,24},{1,5},{5... | collective-permute-start | bytes 208904 | tf_op jit(solution)/shard_map/ppermute | solution.py:436
  61.2 9.1 %collective-permute-start.15 = (bf16[1088,128]{1,0:T(8,128)(2,1)S(1)}, bf16[1088,128]{1,0:T(8,128)(2,1)S(1)}, u32[]{:S(2)}, u32[]{:S(2)}) collective-permute-start(bf16[1088,128]{1,0:T(8,128)(2,1)S(1)} %get-tuple-element.60), channel_id=1, source_target_pairs={{0,1},{1,0},{2,3},{3,2},{4,5},{5,4},{6,7},{7,6},{8,9},{9,8},{10,11... | collective-permute-start | bytes 835592 | tf_op jit(solution)/shard_map/ppermute | solution.py:436
  61.3 6.6 %collective-permute-start.16 = (bf16[544,128]{1,0:T(8,128)(2,1)S(1)}, bf16[544,128]{1,0:T(8,128)(2,1)S(1)}, u32[]{:S(2)}, u32[]{:S(2)}) collective-permute-start(bf16[544,128]{1,0:T(8,128)(2,1)S(1)} %shard_map.94.mine_ref), channel_id=1, source_target_pairs={{0,2},{1,3},{2,0},{3,1},{4,6},{5,7},{6,4},{7,5},{8,10},{9,11},{10,... | collective-permute-start | bytes 417800 | tf_op jit(solution)/shard_map/ppermute | solution.py:436
  62.9 7.5 %collective-permute-start.17 = (bf16[544,128]{1,0:T(8,128)(2,1)S(1)}, bf16[544,128]{1,0:T(8,128)(2,1)S(1)}, u32[]{:S(2)}, u32[]{:S(2)}) collective-permute-start(bf16[544,128]{1,0:T(8,128)(2,1)S(1)} %get-tuple-element.59.others_ref), channel_id=1, source_target_pairs={{0,2},{1,3},{2,0},{3,1},{4,6},{5,7},{6,4},{7,5},{8,10},{9,11},{10,... | collective-permute-start | bytes 417800 | tf_op jit(solution)/shard_map/ppermute | solution.py:436
  67.9 3.7 %collective-permute-start.18 = (bf16[544,128]{1,0:T(8,128)(2,1)S(1)}, bf16[544,128]{1,0:T(8,128)(2,1)S(1)}, u32[]{:S(2)}, u32[]{:S(2)}) collective-permute-start(bf16[544,128]{1,0:T(8,128)(2,1)S(1)} %collective-permute-done.16.mine_ref), channel_id=1, source_target_pairs={{0,1},{1,0},{2,3},{3,2},{4,5},{5,4},{6,7},{7,6},{8,9},{9,8},{10,11... | collective-permute-start | bytes 417800 | tf_op jit(solution)/shard_map/ppermute | solution.py:436
  70.3 1.4 %collective-permute-start.19 = (bf16[544,128]{1,0:T(8,128)(2,1)S(1)}, bf16[544,128]{1,0:T(8,128)(2,1)S(1)}, u32[]{:S(2)}, u32[]{:S(2)}) collective-permute-start(bf16[544,128]{1,0:T(8,128)(2,1)S(1)} %collective-permute-done.17.others_ref), channel_id=1, source_target_pairs={{0,1},{1,0},{2,3},{3,2},{4,5},{5,4},{6,7},{7,6},{8,9},{9,8},{10,11... | collective-permute-start | bytes 417800 | tf_op jit(solution)/shard_map/ppermute | solution.py:436
  71.6 20.1 %copy-start.2 = (f32[512,128]{1,0:T(8,128)S(1)}, f32[512,128]{1,0:T(8,128)}, u32[]{:S(2)}) copy-start(f32[512,128]{1,0:T(8,128)} %first_ref.1) | copy-start | bytes 786436
  72.6 1.7 %collective-permute-start.20 = (bf16[272,512]{1,0:T(8,128)(2,1)S(1)}, bf16[272,512]{1,0:T(8,128)(2,1)S(1)}, u32[]{:S(2)}, u32[]{:S(2)}) collective-permute-start(bf16[272,512]{1,0:T(8,128)(2,1)S(1)} %get-tuple-element.68), channel_id=1, source_target_pairs={{0,1},{1,0},{2,3},{3,2},{4,5},{5,4},{6,7},{7,6},{8,9},{9,8},{10,11... | collective-permute-start | bytes 835592 | tf_op jit(solution)/shard_map/ppermute | solution.py:436
  74.3 4.5 %collective-permute-start.21 = (bf16[272,128]{1,0:T(8,128)(2,1)S(1)}, bf16[272,128]{1,0:T(8,128)(2,1)S(1)}, u32[]{:S(2)}, u32[]{:S(2)}) collective-permute-start(bf16[272,128]{1,0:T(8,128)(2,1)S(1)} %get-tuple-element.70), channel_id=1, source_target_pairs={{0,4},{4,0},{8,12},{12,8},{16,20},{20,16},{24,28},{28,24},{1,5},{5... | collective-permute-start | bytes 208904 | tf_op jit(solution)/shard_map/ppermute | solution.py:436
  75.0 4.3 %collective-permute-start.24 = (bf16[256,128]{1,0:T(8,128)(2,1)S(1)}, bf16[256,128]{1,0:T(8,128)(2,1)S(1)}, u32[]{:S(2)}, u32[]{:S(2)}) collective-permute-start(bf16[256,128]{1,0:T(8,128)(2,1)S(1)} %get-tuple-element.74), channel_id=1, source_target_pairs={{0,8},{4,12},{8,0},{12,4},{16,24},{20,28},{24,16},{28,20},{1,9},{5... | collective-permute-start | bytes 196616 | tf_op jit(solution)/shard_map/ppermute | solution.py:436
  78.9 4.4 %collective-permute-start.22 = (bf16[272,128]{1,0:T(8,128)(2,1)S(1)}, bf16[272,128]{1,0:T(8,128)(2,1)S(1)}, u32[]{:S(2)}, u32[]{:S(2)}) collective-permute-start(bf16[272,128]{1,0:T(8,128)(2,1)S(1)} %shard_map.101.mine_ref), channel_id=1, source_target_pairs={{0,8},{4,12},{8,0},{12,4},{16,24},{20,28},{24,16},{28,20},{1,9},{5... | collective-permute-start | bytes 208904 | tf_op jit(solution)/shard_map/ppermute | solution.py:436
  79.3 5.8 %collective-permute-start.25 = (bf16[256,128]{1,0:T(8,128)(2,1)S(1)}, bf16[256,128]{1,0:T(8,128)(2,1)S(1)}, u32[]{:S(2)}, u32[]{:S(2)}) collective-permute-start(bf16[256,128]{1,0:T(8,128)(2,1)S(1)} %shard_map.104.mine_ref), channel_id=1, source_target_pairs={{0,4},{4,0},{8,12},{12,8},{16,20},{20,16},{24,28},{28,24},{1,5},{5... | collective-permute-start | bytes 196616 | tf_op jit(solution)/shard_map/ppermute | solution.py:436
  83.3 6.1 %collective-permute-start.23 = (bf16[272,128]{1,0:T(8,128)(2,1)S(1)}, bf16[272,128]{1,0:T(8,128)(2,1)S(1)}, u32[]{:S(2)}, u32[]{:S(2)}) collective-permute-start(bf16[272,128]{1,0:T(8,128)(2,1)S(1)} %shard_map.102.mine_ref), channel_id=1, source_target_pairs={{0,16},{4,20},{8,24},{12,28},{16,0},{20,4},{24,8},{28,12},{1,17},{... | collective-permute-start | bytes 208904 | tf_op jit(solution)/shard_map/ppermute | solution.py:436
  85.1 5.7 %collective-permute-start.26 = (bf16[256,128]{1,0:T(8,128)(2,1)S(1)}, bf16[256,128]{1,0:T(8,128)(2,1)S(1)}, u32[]{:S(2)}, u32[]{:S(2)}) collective-permute-start(bf16[256,128]{1,0:T(8,128)(2,1)S(1)} %shard_map.105.mine_ref), channel_id=1, source_target_pairs={{0,16},{4,20},{8,24},{12,28},{16,0},{20,4},{24,8},{28,12},{1,17},{... | collective-permute-start | bytes 196616 | tf_op jit(solution)/shard_map/ppermute | solution.py:436
  86.4 5.3 %collective-permute-start.29 = (f32[256,128]{1,0:T(8,128)S(1)}, f32[256,128]{1,0:T(8,128)S(1)}, u32[]{:S(2)}, u32[]{:S(2)}) collective-permute-start(f32[256,128]{1,0:T(8,128)S(1)} %get-tuple-element.77), channel_id=1, source_target_pairs={{0,1},{1,0},{2,3},{3,2},{4,5},{5,4},{6,7},{7,6},{8,9},{9,8},{10,11... | collective-permute-start | bytes 393224 | tf_op jit(solution)/shard_map/ppermute | solution.py:436
  90.9 5.0 %collective-permute-start.28 = (f32[256,128]{1,0:T(8,128)S(1)}, f32[256,128]{1,0:T(8,128)S(1)}, u32[]{:S(2)}, u32[]{:S(2)}) collective-permute-start(f32[256,128]{1,0:T(8,128)S(1)} %shard_map.106.mine_b), channel_id=1, source_target_pairs={{0,8},{4,12},{8,0},{12,4},{16,24},{20,28},{24,16},{28,20},{1,9},{5... | collective-permute-start | bytes 393224 | tf_op jit(solution)/shard_map/ppermute | solution.py:436
  90.9 5.0 %collective-permute-start.27 = (f32[256,128]{1,0:T(8,128)S(1)}, f32[256,128]{1,0:T(8,128)S(1)}, u32[]{:S(2)}, u32[]{:S(2)}) collective-permute-start(f32[256,128]{1,0:T(8,128)S(1)} %get-tuple-element.71.mine_a), channel_id=1, source_target_pairs={{0,4},{4,0},{8,12},{12,8},{16,20},{20,16},{24,28},{28,24},{1,5},{5... | collective-permute-start | bytes 393224 | tf_op jit(solution)/shard_map/ppermute | solution.py:436
